TPU v7x, 128 devices: a whole 4x4x4 slice. The times are simulated.
128 devices in a mesh: dp: 2 (over x_lo), space: 64 (over z, y, x_hi, core).
Axes of the slice: x: 4 (x_hi: 2, x_lo: 2; x = x_hi * 2 + x_lo), y: 4, z: 4, core: 2. Of those that a mesh axis runs over, the one named last changes fastest.
Arguments:
- stash: bfloat16 [64, 64, 4, 2160], P('space', None, 'dp'), may hold values from -5 to 5
- piece_map: int32 [64, 64], P(None, 'space'), may hold values from 0 to 63, as said below
- gain_one: float32 [768], replicated, may hold values from 0.5 to 1.5
- spec_one: float32 [2, 8, 96, 96], replicated, may hold values from -0.4375 to 0.4375
- bias_one: float32 [2, 768], replicated, may hold values from -3 to 3
- spec_two: float32 [2, 8, 96, 96], replicated, may hold values from -0.4375 to 0.4375
- bias_two: float32 [2, 768], replicated, may hold values from -0.6 to 0.6
- gain_two: float32 [768], replicated, may hold values from 0.5 to 1.5
- fc_one: bfloat16 [768, 3072], replicated, may hold values from -0.21875 to 0.21875
- bias_fc: float32 [3072], replicated, may hold values from -3 to 3
- fc_two: bfloat16 [3072, 768], replicated, may hold values from -0.109375 to 0.109375
- cotangent: bfloat16 [4, 64, 180, 768], P('dp', 'space'), may hold values from -6 to 6
Outputs:
- grad_input: float32 [4, 64, 180, 768], P('dp', 'space')
- grad_fc_one: float32 [768, 3072], P(None, ('dp', 'space'))
- grad_fc_two: float32 [3072, 768], P(('dp', 'space'))
- grad_bias_fc: float32 [3072], replicated
- grad_bias_out: float32 [768], replicated
- grad_gain_one: float32 [768], replicated
- grad_gain_two: float32 [768], replicated
- grad_spec_one: float32 [2, 8, 96, 96], replicated
- grad_bias_one: float32 [2, 768], replicated
- grad_spec_two: float32 [2, 8, 96, 96], replicated
- grad_bias_two: float32 [2, 768], replicated
Inputs may be any that keep to these rules, and one draw needn't show every extreme that they name: `piece_map`: each column holds every number from 0 to 63 once.
All inputs are finite; a program needn't handle non-finite values.
Results may differ from a plain program's by a relative error of at most 0.0046.
Values may be sent and summed in bfloat16 or wider, within the bound.
No kernel may reach another device: no remote copies, remote signals or barrier semaphores. Data moves between devices by JAX's collectives and lax.ppermute only.
A program may use at most 128 MiB of HBM per device.

v0:
```python
import math

import jax
import jax.numpy as jnp
import numpy as np
from jax import lax
from jax.experimental import pallas as pl
from jax.experimental.pallas import tpu as pltpu
from jax.sharding import Mesh, PartitionSpec as P

KW = 64
SPACE = ("z", "y", "xh", "c")
EVERY = ("dp",) + SPACE

epsilon = 1e-05
bf16 = jnp.bfloat16
f32 = jnp.float32
ROOT = math.sqrt(2.0 / math.pi)
CUBE = 0.044715


def exchange(values, axes):
    return lax.all_to_all(values, axes, split_axis=0, concat_axis=0, tiled=True)


def high_low(table):
    table = np.asarray(table, np.float32)
    high = table.astype(bf16)
    low = (table - high.astype(np.float32)).astype(bf16)
    return np.stack((high, low))


def zonal_tables(samples, lon):
    angle = 2.0 * np.pi * (np.outer(np.arange(KW), np.arange(lon)) % lon) / lon
    both = np.stack((np.cos(angle), -np.sin(angle)), axis=1) / math.sqrt(lon)
    eye = np.eye(samples)
    plain = np.einsum("krw,ab->krabw", both, eye)
    plain = plain.reshape(KW * 2 * samples, samples * lon)
    double = np.where(np.arange(KW) == 0, 1.0, 2.0)
    doubled = plain * np.repeat(double, 2 * samples)[:, None]
    return plain, doubled


def meridian_table(samples, lat):
    angle = 2.0 * np.pi * (np.outer(np.arange(lat), np.arange(lat)) % lat) / lat
    cos, sin = np.cos(angle) / math.sqrt(lat), np.sin(angle) / math.sqrt(lat)
    turn = np.stack((np.stack((cos, sin), -1), np.stack((-sin, cos), -1)))
    whole = np.einsum("qksr,ab->qkasrb", turn, np.eye(samples))
    return whole.reshape(2 * lat * samples, lat * 2 * samples)


def dot(a, b, ca=1, cb=0):
    return lax.dot_general(a, b, (((ca,), (cb,)), ((), ())), preferred_element_type=f32)


def split(a):
    high = a.astype(bf16)
    return high, (a - high.astype(f32)).astype(bf16)


def dot3(a, b, ca=1, cb=0):
    return dot(a[0], b[0], ca, cb) + (dot(a[1], b[0], ca, cb) + dot(a[0], b[1], ca, cb))


def dot2(table, b):
    return dot(table[0], b) + dot(table[1], b)


def bend(x):
    return jnp.tanh(ROOT * (x + CUBE * (x * x * x)))


def smooth_gate(x):
    return 0.5 * x * (1.0 + bend(x))


def gate_slope(x):
    t = bend(x)
    return 0.5 * (1.0 + t) + (0.5 * x) * (1.0 - t * t) * (ROOT * (1.0 + (3.0 * CUBE) * (x * x)))


def normalise(x):
    centred = x - jnp.mean(x, axis=-1, keepdims=True)
    rstd = lax.rsqrt(jnp.mean(centred * centred, axis=-1, keepdims=True) + epsilon)
    return centred * rstd, rstd


def norm_pull(grad, gain, xhat, rstd):
    scaled = grad * gain
    return rstd * (
        scaled
        - jnp.mean(scaled, axis=-1, keepdims=True)
        - xhat * jnp.mean(scaled * xhat, axis=-1, keepdims=True)
    )


def to_rows(block):
    return block.astype(f32).reshape(block.shape[0] * block.shape[1], block.shape[2]).astype(bf16)


def to_pieces(values):
    return values.reshape(values.shape[0] // 4, 4, values.shape[1]).astype(bf16)


def project(values, table_ref, out_ref):
    half = out_ref.shape[2]
    ranks = out_ref.shape[0] // 2
    found = dot3((table_ref[0], table_ref[1]), split(values))
    out_ref[:ranks] = to_pieces(found[:, :half])
    out_ref[ranks:] = to_pieces(found[:, half:])


def expand(rows_ref, table_ref):
    ranks = rows_ref.shape[0] // 2
    table = (table_ref[0], table_ref[1])
    return jnp.concatenate(
        [dot2(table, to_rows(rows_ref[ranks * h : ranks * (h + 1), :4])) for h in range(2)], axis=1
    )


def first_kernel(base_ref, table_ref, sent_ref, xhat_ref, rstd_ref):
    xhat, rstd = normalise(base_ref[...])
    xhat_ref[...] = xhat
    rstd_ref[...] = jnp.broadcast_to(rstd, rstd_ref.shape)
    project(xhat, table_ref, sent_ref)


def field_kernel(rows_ref, table_ref, base_ref, xhat_ref, gains_ref, flat_ref, xhat2_ref, rstd2_ref):
    mixed = base_ref[...] + xhat_ref[...] * gains_ref[0:1] + expand(rows_ref, table_ref)
    xhat2, rstd2 = normalise(mixed)
    xhat2_ref[...] = xhat2
    rstd2_ref[...] = jnp.broadcast_to(rstd2, rstd2_ref.shape)
    flat_ref[...] = (xhat2 * gains_ref[1:2]).astype(bf16)


def back_kernel(
    grad_ref, cot_ref, xhat2_ref, rstd2_ref, xhat_ref, gains_ref, table_ref, sent_ref, mixed_ref, sums_ref
):
    grad = grad_ref[...]
    xhat2 = xhat2_ref[...]
    cot = cot_ref[...].astype(f32)
    mixed = cot + norm_pull(grad, gains_ref[1:2], xhat2, rstd2_ref[:, 0:1])
    mixed_ref[...] = mixed
    sums_ref[0:1] = jnp.sum(cot, axis=0, keepdims=True)
    sums_ref[1:2] = jnp.sum(mixed * xhat_ref[...], axis=0, keepdims=True)
    sums_ref[2:3] = jnp.sum(grad * xhat2, axis=0, keepdims=True)
    project(mixed, table_ref, sent_ref)


def last_kernel(rows_ref, table_ref, mixed_ref, xhat_ref, rstd_ref, gains_ref, out_ref):
    mixed = mixed_ref[...]
    grad = mixed + expand(rows_ref, table_ref)
    result = mixed + norm_pull(grad, gains_ref[0:1], xhat_ref[...], rstd_ref[:, 0:1])
    out_ref[:, 0] = result


def hidden_kernel(
    place_ref, flat_ref, cot_ref, one_ref, bias_ref, two_ref, grad_ref, active_ref, tall_ref, sum_ref
):
    pre = dot(flat_ref[...], one_ref[...]) + bias_ref[...]
    up = dot(cot_ref[...], two_ref[...], 1, 1)
    t = bend(pre)
    half = 0.5 * (1.0 + t)
    active = pre * half
    grad = up * (half + (0.5 * pre) * (1.0 - t * t) * (ROOT + (3.0 * CUBE * ROOT) * (pre * pre)))
    grad_ref[...] = grad.astype(bf16)
    active_ref[...] = active.astype(bf16)
    tall_ref[...] = jnp.where(place_ref[3] == 0, active, grad).astype(bf16)
    sum_ref[0] = jnp.sum(grad, axis=0, keepdims=True)


def mix(real, imag, weights, index):
    wr = (weights[0, index], weights[1, index])
    wi = (weights[0, index + 1], weights[1, index + 1])
    real, imag = split(real), split(imag)
    return dot3(real, wr) - dot3(imag, wi), dot3(real, wi) + dot3(imag, wr)


def mix_pull(real, imag, weights, index):
    wr = (weights[0, index], weights[1, index])
    wi = (weights[0, index + 1], weights[1, index + 1])
    return (
        dot3(real, wr, 1, 1) + dot3(imag, wi, 1, 1),
        dot3(imag, wr, 1, 1) - dot3(real, wi, 1, 1),
    )


def compact(full, inner):
    lane = lax.broadcasted_iota(jnp.int32, (inner, full.shape[1]), 1)
    kept = None
    for j in range(full.shape[0] // inner):
        here = (lane >= inner * j) & (lane < inner * (j + 1))
        part = jnp.where(here, full[inner * j : inner * (j + 1)], 0.0)
        kept = part if kept is None else kept + part
    return kept


def spectral_kernel(rows_ref, table_ref, turned_ref, weights_ref, vectors_ref, sent_ref, plain_ref, pre_ref):
    ranks = rows_ref.shape[0] // 2
    half = 2 * ranks
    table = (table_ref[0], table_ref[1])
    for dp in range(2):
        found = dot2(table, to_rows(rows_ref[ranks * dp : ranks * (dp + 1)]))
        plain_ref[0, half * dp : half * (dp + 1)] = found[:half]
        plain_ref[1, half * dp : half * (dp + 1)] = found[half:]
    gain = vectors_ref[0:1]
    real, imag = mix(plain_ref[0] * gain, plain_ref[1] * gain, weights_ref, 0)
    real = real + vectors_ref[1:2]
    imag = imag + vectors_ref[2:3]
    pre_ref[0] = real
    pre_ref[1] = imag
    real, imag = mix(smooth_gate(real), smooth_gate(imag), weights_ref, 2)
    real = real + vectors_ref[3:4]
    imag = imag + vectors_ref[4:5]
    turned = (turned_ref[0], turned_ref[1])
    for dp in range(2):
        both = jnp.concatenate(
            (real[half * dp : half * (dp + 1)], imag[half * dp : half * (dp + 1)]), axis=0
        )
        sent_ref[ranks * dp : ranks * (dp + 1)] = to_pieces(dot3(turned, split(both)))


def spectral_back_kernel(
    rows_ref,
    table_ref,
    turned_ref,
    weights_ref,
    vectors_ref,
    plain_ref,
    pre_ref,
    lines_ref,
    place_ref,
    packet_ref,
    grads_ref,
    sums_ref,
    work_ref,
):
    ranks = rows_ref.shape[0] // 2
    half = 2 * ranks
    inner = grads_ref.shape[0] // 4
    table = (table_ref[0], table_ref[1])
    found = [
        dot2(table, to_rows(rows_ref[ranks * dp : ranks * (dp + 1)])) for dp in range(2)
    ]
    real = jnp.concatenate((found[0][:half], found[1][:half]), axis=0)
    imag = jnp.concatenate((found[0][half:], found[1][half:]), axis=0)

    def weight_grads(first, second, grad_real, grad_imag, at):
        grads_ref[inner * at : inner * (at + 1)] = compact(
            dot3(first, grad_real, 0, 0) + dot3(second, grad_imag, 0, 0), inner
        )
        grads_ref[inner * (at + 1) : inner * (at + 2)] = compact(
            dot3(first, grad_imag, 0, 0) - dot3(second, grad_real, 0, 0), inner
        )

    sums_ref[3:4] = jnp.sum(real, axis=0, keepdims=True)
    sums_ref[4:5] = jnp.sum(imag, axis=0, keepdims=True)
    pre_real, pre_imag = pre_ref[0], pre_ref[1]
    real, imag = split(real), split(imag)
    weight_grads(split(smooth_gate(pre_real)), split(smooth_gate(pre_imag)), real, imag, 2)
    real, imag = mix_pull(real, imag, weights_ref, 2)
    real = real * gate_slope(pre_real)
    imag = imag * gate_slope(pre_imag)
    sums_ref[1:2] = jnp.sum(real, axis=0, keepdims=True)
    sums_ref[2:3] = jnp.sum(imag, axis=0, keepdims=True)
    gain = vectors_ref[0:1]
    real, imag = split(real), split(imag)
    plain_real, plain_imag = plain_ref[0], plain_ref[1]
    weight_grads(split(plain_real * gain), split(plain_imag * gain), real, imag, 0)
    real, imag = mix_pull(real, imag, weights_ref, 0)
    sums_ref[0:1] = jnp.sum(real * plain_real + imag * plain_imag, axis=0, keepdims=True)
    turned = (turned_ref[0], turned_ref[1])
    for dp in range(2):
        both = jnp.concatenate(
            (real[half * dp : half * (dp + 1)], imag[half * dp : half * (dp + 1)]), axis=0
        )
        found = dot3(turned, split(both))
        work_ref[ranks * dp : ranks * (dp + 1), 0:4] = found.reshape(ranks, 4, found.shape[1])
    total = 2 * ranks
    for r in range(3):
        work_ref[:, 4 + r] = grads_ref[total * r : total * (r + 1)]
    known = lines_ref.shape[0]
    work_ref[:, 7] = jnp.zeros((total, found.shape[1]), f32)
    work_ref[:known, 7] = lines_ref[...]
    for h in range(2):

        @pl.when(place_ref[6] == h)
        def _(h=h):
            work_ref[known + 5 * h : known + 5 * h + 5, 7] = sums_ref[...]

    packet_ref[...] = work_ref[...].astype(bf16)


def unpack_kernel(spread_ref, one_ref, two_ref, fc_ref, out_ref, gain1_ref, gain2_ref, b1_ref, b2_ref, work_ref):
    total = spread_ref.shape[0]
    inner = one_ref.shape[2]
    wide = spread_ref[...].astype(f32)
    for h in range(2):
        for r in range(3):
            work_ref[h, total * r : total * (r + 1)] = wide[:, 3 * h + r]
        for m in range(4):
            for j in range(4):
                (one_ref, two_ref)[m // 2][m % 2, 4 * h + j] = work_ref[
                    h, inner * m : inner * (m + 1), inner * j : inner * (j + 1)
                ]
    lines = wide[:24, 6]

    def joined(*rows):
        return jnp.concatenate([lines[r : r + 1] for r in rows], axis=1)

    fc_ref[...] = joined(*range(8))
    out_ref[...] = joined(8, 9)
    gain1_ref[...] = joined(10, 11) + joined(14, 19)
    gain2_ref[...] = joined(12, 13)
    for i in range(2):
        b1_ref[i : i + 1] = joined(15 + i, 20 + i)
        b2_ref[i : i + 1] = joined(17 + i, 22 + i)


def whole(shape):
    zeros = (0,) * len(shape)
    return pl.BlockSpec(shape, lambda *_: zeros)


def call(kernel, outs, *args, grant=16, grid=(1,), in_specs=None, out_specs=None, free=(), free_outs=(), **more):
    in_specs = in_specs or [whole(a.shape) for a in args]
    return pl.pallas_call(
        kernel,
        out_shape=[
            (jax.ShapeDtypeStruct if i in free_outs else pltpu.HBM)(shape, kind)
            for i, (shape, kind) in enumerate(outs)
        ],
        compiler_params=pltpu.CompilerParams(vmem_limit_bytes=grant << 20),
        grid=grid,
        in_specs=in_specs,
        out_specs=out_specs or [whole(shape) for shape, _ in outs],
        **more,
    )(
        *(
            a if spec is SMEM or i in free else pltpu.with_memory_space_constraint(a, pltpu.HBM)
            for i, (a, spec) in enumerate(zip(args, in_specs))
        )
    )


SMEM = pl.BlockSpec(memory_space=pltpu.SMEM)


def weight_kernel(
    place_ref,
    grad_ref,
    active_ref,
    flat_ref,
    cot_ref,
    tall_ref,
    wide_ref,
    own_ref,
    out1_ref,
    out2_ref,
    out3_ref,
    acc_ref,
):
    step = pl.program_id(0)
    low, at_z = step // 4, step % 4
    share = own_ref.shape[1]
    x, y, core = place_ref[0], place_ref[1], place_ref[3]
    first = core == 0

    @pl.when(first)
    def _():
        acc_ref[...] = dot(grad_ref[...], flat_ref[...], 0, 0)

    @pl.when(core == 1)
    def _():
        acc_ref[...] = dot(active_ref[...], cot_ref[...], 0, 0)

    acc_ref[...] += dot(tall_ref[...], wide_ref[...], 0, 0)
    for at_y in range(4):
        for at_xh in range(2):
            at_x = 2 * at_xh + low
            at = (at_y * 2 + at_xh) * share
            far = jnp.where(first, at_x - x, at_y - y) & 3
            spot = jnp.where(first, at_y * 4 + at_z, at_z * 4 + at_x)
            for r, ref in enumerate((own_ref, out1_ref, out2_ref, out3_ref)):

                @pl.when(far == r)
                def _(ref=ref, at=at, spot=spot):
                    ref[spot] = acc_ref[at : at + share].astype(ref.dtype)


def plane_kernel(place_ref, own_in_ref, *refs):
    got, own_ref, outs = refs[:3], refs[3], refs[4:]
    for d in range(4):
        for i in range(4):
            at = 4 * ((place_ref[4] + d) & 3) + i
            total = own_in_ref[at]
            for r in range(3):
                total = total + got[r][at].astype(f32)
            if d == 0:
                own_ref[i] = total
            else:
                outs[d - 1][i] = total.astype(bf16)


def line_kernel(place_ref, own_in_ref, *refs):
    got, own_ref, outs = refs[:3], refs[3], refs[4:]
    for d in range(4):
        at = (place_ref[5] + d) & 3
        total = own_in_ref[at]
        for r in range(3):
            total = total + got[r][at].astype(f32)
        if d == 0:
            own_ref[...] = total
        else:
            outs[d - 1][...] = total.astype(bf16)


def point_kernel(scale, place_ref, own_ref, *refs):
    got, kept_ref, send_ref = refs[:3], refs[3], refs[4]
    share = kept_ref.shape[0]
    total = own_ref[...]
    for r in range(3):
        total = total + got[r][...].astype(f32)
    total = total * scale
    first = place_ref[3] == 0
    kept_ref[...] = jnp.where(first, total[:share], total[share:])
    send_ref[...] = jnp.where(first, total[share:], total[:share])


def neighbours(stage, far):
    pairs = []
    for rank in range(128):
        core, xh, y, z, low = rank & 1, (rank >> 1) & 1, (rank >> 2) & 3, (rank >> 4) & 3, rank >> 6
        at = [2 * xh + low, y, z]
        axis = (stage + core) % 3
        at[axis] = (at[axis] + far) & 3
        x, y, z = at
        pairs.append((rank, ((x & 1) << 6) | (z << 4) | (y << 2) | ((x >> 1) << 1) | core))
    return pairs


def send_all(pieces, stage):
    return [lax.ppermute(pieces[r], EVERY, neighbours(stage, r + 1)) for r in range(3)]


def after(value, others):
    return lax.optimization_barrier((value, others))[0]


def weight_place():
    core = lax.axis_index("c")
    x = 2 * lax.axis_index("xh") + lax.axis_index("dp")
    y, z = lax.axis_index("y"), lax.axis_index("z")
    first = core == 0
    return jnp.stack(
        (x, y, z, core, jnp.where(first, y, z), jnp.where(first, z, x), lax.axis_index("dp"))
    ).astype(
        jnp.int32
    )


def swap(values):
    return lax.ppermute(values, "c", [(0, 1), (1, 0)])


def weight_start(place, grad_hidden, active, flat, cot, tall):
    tokens, hidden = grad_hidden.shape
    width = flat.shape[1]
    first = place[3] == 0
    tall = swap(tall)
    wide = swap(jnp.where(first, cot, flat))
    cube = (16, hidden // 64, width)
    ahead = pl.BlockSpec((tokens, hidden // 8), lambda g: (0, g))
    across = whole(flat.shape)
    return call(
        weight_kernel,
        [(cube, f32)] + [(cube, bf16)] * 3,
        place,
        grad_hidden,
        active,
        flat,
        cot,
        tall,
        wide,
        grant=24,
        grid=(8,),
        in_specs=[SMEM, ahead, ahead, across, across, ahead, across],
        out_specs=[whole(cube)] * 4,
        scratch_shapes=[pltpu.VMEM((hidden // 8, width), f32)],
        free=range(1, 7),
        cost_estimate=pl.CostEstimate(
            flops=4 * tokens * hidden * width, bytes_accessed=14 << 20, transcendentals=0
        ),
    )


def weight_second(place, own, got):
    cube = own.shape
    row = (4,) + cube[1:]
    return call(
        plane_kernel,
        [(row, f32)] + [(row, bf16)] * 3,
        place,
        own,
        *got,
        grid=(1,),
        in_specs=[SMEM] + [whole(cube)] * 4,
        out_specs=[whole(row)] * 4,
        free=range(5),
        free_outs=range(4),
    )


def weight_third(place, own, got):
    row = own.shape
    line = row[1:]
    return call(
        line_kernel,
        [(line, f32)] + [(line, bf16)] * 3,
        place,
        own,
        *got,
        grid=(1,),
        in_specs=[SMEM, whole(row)] + [whole(row)] * 3,
        out_specs=[whole(line)] * 4,
        free=range(5),
        free_outs=range(4),
    )


def block_diagonal(weights):
    blocks, inner = weights.shape[1:3]
    tall = weights.reshape(2, blocks * inner, inner)
    wide = jnp.concatenate((tall,) * blocks, axis=2)
    row = lax.broadcasted_iota(jnp.int32, wide.shape, 1) // inner
    lane = lax.broadcasted_iota(jnp.int32, wide.shape, 2) // inner
    return jnp.where(row == lane, wide, 0.0)


def local(
    stash,
    piece_map,
    gain_one,
    spec_one,
    bias_one,
    spec_two,
    bias_two,
    gain_two,
    fc_one,
    bias_fc,
    fc_two,
    cotangent,
):
    samples, _, lon_cells, width = cotangent.shape
    lat_total = lax.axis_size(SPACE)
    ranks = lax.axis_size(EVERY)
    tokens = samples * lon_cells
    hidden = fc_one.shape[1]
    half = width // 2
    rows = 4 * ranks
    piece = (ranks, 4, half)
    plain_table, doubled_table = zonal_tables(samples, lon_cells)
    meridian = meridian_table(samples, lat_total)
    down, back_down = high_low(plain_table), high_low(doubled_table)
    up, back_up = high_low(plain_table.T), high_low(doubled_table.T)
    forward, inverse = high_low(meridian), high_low(meridian.T)

    arrived = exchange(stash[0], SPACE)
    ordering = jnp.argsort(piece_map[:, 0])
    placed = jnp.take(arrived, ordering, axis=0)
    base = jnp.transpose(placed, (1, 0, 2)).reshape(tokens, width).astype(f32)
    upstream = cotangent.reshape(tokens, width)
    gains = jnp.stack((gain_one, gain_two))

    which = lax.axis_index("dp")
    blocks, inner = spec_one.shape[1:3]
    mine = blocks // 2
    both = jnp.concatenate(
        [
            block_diagonal(lax.dynamic_slice_in_dim(w, which * mine, mine, 1))
            for w in (spec_one, spec_two)
        ]
    )
    weights = jnp.stack(split(both))
    vectors = lax.dynamic_slice_in_dim(
        jnp.concatenate((gain_one[None], bias_one, bias_two)), which * half, half, 1
    )

    sent, xhat, rstd = call(
        first_kernel,
        [(piece, bf16), ((tokens, width), f32), ((tokens, 128), f32)],
        base,
        down,
        free=(0,),
    )
    got = exchange(sent, EVERY)
    sent, plain, pre = call(
        spectral_kernel,
        [(piece, bf16), ((2, rows // 2, half), f32), ((2, rows // 2, half), f32)],
        got,
        forward,
        inverse,
        weights,
        vectors,
        free=(0,),
    )
    got = exchange(sent, EVERY)
    normed_flat, xhat2, rstd2 = call(
        field_kernel,
        [((tokens, width), bf16), ((tokens, width), f32), ((tokens, 128), f32)],
        got,
        back_up,
        base,
        xhat,
        gains,
        free=(0,),
        free_outs=(0,),
    )
    place = weight_place()
    block = (tokens, hidden // 8)
    across = pl.BlockSpec(block, lambda g: (0, g))
    grad_hidden_flat, active_flat, tall, bias_sum = call(
        hidden_kernel,
        [((tokens, hidden), bf16)] * 3 + [((8, 1, hidden // 8), f32)],
        place,
        normed_flat,
        upstream,
        fc_one,
        bias_fc.reshape(1, hidden),
        fc_two,
        grid=(8,),
        in_specs=[
            SMEM,
            whole(normed_flat.shape),
            whole(upstream.shape),
            pl.BlockSpec((width, hidden // 8), lambda g: (0, g)),
            pl.BlockSpec((1, hidden // 8), lambda g: (0, g)),
            pl.BlockSpec((hidden // 8, width), lambda g: (g, 0)),
        ],
        out_specs=[across] * 3 + [pl.BlockSpec((1, 1, hidden // 8), lambda g: (g, 0, 0))],
        free=(1, 2, 4),
        free_outs=(0, 1, 3),
        cost_estimate=pl.CostEstimate(
            flops=4 * tokens * hidden * width,
            bytes_accessed=18 << 20,
            transcendentals=tokens * hidden,
        ),
    )
    grad_normed_two = jnp.einsum("tf,df->td", grad_hidden_flat, fc_one, preferred_element_type=f32)
    sent, grad_mixed, sums = call(
        back_kernel,
        [(piece, bf16), ((tokens, width), f32), ((3, width), f32)],
        grad_normed_two,
        upstream,
        xhat2,
        rstd2,
        xhat,
        gains,
        back_down,
        free=(0, 1),
    )
    got = exchange(sent, EVERY)

    grad_scale = 1.0 / math.sqrt(samples * lax.axis_size("dp") * lat_total * lon_cells)
    own, *sent = weight_start(
        place, grad_hidden_flat, active_flat, normed_flat, upstream, tall
    )
    first_got = send_all(sent, 0)
    got = after(got, sent)

    lines = jnp.concatenate((bias_sum.reshape(-1, half), sums.reshape(-1, half)))
    matrices = (4 * inner, half)
    (packet,) = call(
        spectral_back_kernel,
        [((ranks, 8, half), bf16)],
        got,
        forward,
        inverse,
        weights,
        vectors,
        plain,
        pre,
        lines,
        place,
        in_specs=[whole(a.shape) for a in (got, forward, inverse, weights, vectors, plain, pre)]
        + [whole(lines.shape), SMEM],
        scratch_shapes=[
            pltpu.VMEM(matrices, f32),
            pltpu.VMEM((5, half), f32),
            pltpu.VMEM((ranks, 8, half), f32),
        ],
        free=(0, 7, 8),
        grant=20,
    )
    got = exchange(packet, EVERY)
    own, *sent = weight_second(place, own, first_got)
    second_got = send_all(sent, 1)
    (grad_input,) = call(
        last_kernel,
        [((tokens, 1, width), f32)],
        after(got, sent),
        up,
        grad_mixed,
        xhat,
        rstd,
        gains,
        free=(0,),
    )
    sides = jnp.sum(got[:, 4:].reshape(2, ranks // 2, 4, half).astype(f32), axis=1)
    total = jnp.concatenate(
        (sides[0, :3], sides[1, :3], sides[0, 3:] + sides[1, 3:], jnp.zeros((1, half), f32))
    )
    total = (total * grad_scale).astype(bf16)
    spread = exchange(jnp.broadcast_to(total, (ranks,) + total.shape), EVERY)
    own, *sent = weight_third(place, after(own, grad_input), second_got)
    third_got = send_all(sent, 2)
    spread = after(spread, sent)
    whole_spec = spec_one.shape
    unpacked = call(
        unpack_kernel,
        [
            (whole_spec, f32),
            (whole_spec, f32),
            ((1, hidden), f32),
            ((1, width), f32),
            ((1, width), f32),
            ((1, width), f32),
            ((2, width), f32),
            ((2, width), f32),
        ],
        spread,
        scratch_shapes=[pltpu.VMEM((2,) + matrices, f32)],
        free=(0,),
    )
    spec_one_grad, spec_two_grad, fc_grad, out_grad, gain1, gain2, bias1, bias2 = unpacked
    kept, away = call(
        lambda *refs: point_kernel(grad_scale, *refs),
        [((hidden // ranks, width), f32)] * 2,
        place,
        own,
        *third_got,
        in_specs=[SMEM] + [whole(own.shape)] * 4,
        free=range(5),
        free_outs=range(2),
    )
    came = swap(away)
    first = place[3] == 0
    grad_one = jnp.where(first, kept, came)
    grad_two = jnp.where(first, came, kept)
    return (
        grad_input.reshape(samples, lon_cells, 1, width).transpose(0, 2, 1, 3),
        grad_one.T,
        grad_two,
        fc_grad.reshape(hidden),
        out_grad.reshape(width),
        gain1.reshape(width),
        gain2.reshape(width),
        spec_one_grad,
        bias1,
        spec_two_grad,
        bias2,
    )


def solution(mesh):
    fine = Mesh(mesh.devices.reshape(2, 4, 4, 2, 2), EVERY)
    placed = (
        P(SPACE, None, "dp", None),
        P(None, SPACE),
        P(),
        P(),
        P(),
        P(),
        P(),
        P(),
        P(),
        P(),
        P(),
        P("dp", SPACE, None, None),
    )

    return jax.shard_map(
        local,
        mesh=fine,
        in_specs=placed,
        out_specs=(
            P("dp", SPACE, None, None),
            P(None, EVERY),
            P(EVERY, None),
        )
        + (P(),) * 8,
        check_vma=False,
    )
```

profile of v0, /device:TPU:1, one launch (start us, length us, event | category | flops | bytes accessed | tf_op | source)
XLA Modules:
  0.0 214.9 jit_solution(11543849169260334826)
XLA Ops:
  0.7 12.6 %all-to-all-start = ((bf16[64,2,2160]{2,1,0:T(2,128)(2,1)}), bf16[64,2,2160]{2,1,0:T(2,128)(2,1)S(1)}, u32[]{:S(2)}, u32[]{:S(2)}) async-start(bf16[64,2,2160]{2,1,0:T(2,128)(2,1)} %bitcast.43), calls=%async_computation | async-start | bytes 1114112 | tf_op jit(solution)/shard_map/all_to_all | solution.py:23
  13.3 2.7 %sort.17 = (s32[64]{0:T(128)}, s32[64]{0:T(128)S(1)}) sort(s32[64]{0:T(128)} %bitcast.48, s32[64]{0:T(128)S(1)} %iota.40), dimensions={0}, to_apply=%region_0.0 | sort | flops 384 | bytes 1024 | tf_op jit(solution)/shard_map/jit(argsort)/sort | solution.py:569
  16.0 1.0 constant_dynamic-slice_fusion
  17.1 1.3 fusion.1
  18.4 1.3 fusion
  19.7 8.2 %all-to-all-done = bf16[64,2,2160]{2,1,0:T(2,128)(2,1)S(1)} async-done(((bf16[64,2,2160]{2,1,0:T(2,128)(2,1)}), bf16[64,2,2160]{2,1,0:T(2,128)(2,1)S(1)}, u32[]{:S(2)}, u32[]{:S(2)}) %all-to-all-start) | async-done | bytes 552992 | tf_op jit(solution)/shard_map/all_to_all | solution.py:23
  27.9 1.7 gather_fusion
  30.2 1.1 reshape.278.base_ref
  31.4 3.2 %shard_map.257 = (bf16[128,4,384]{2,1,0:T(4,128)(2,1)}, f32[360,768]{1,0:T(8,128)}, f32[360,128]{1,0:T(8,128)}) custom-call(f32[360,768]{1,0:T(8,128)S(1)} %reshape.278.base_ref, bf16[2,256,360]{2,1,0:T(8,128)(2,1)} %constant.80.clone.table_ref), custom_call_target="tpu_custom_call" | custom-call | tf_op jit(solution)/shard_map/pallas_call | solution.py:327
  34.5 3.9 %all-to-all-start.1 = ((bf16[128,4,384]{2,1,0:T(4,128)(2,1)}), bf16[128,4,384]{2,1,0:T(4,128)(2,1)S(1)}, u32[]{:S(2)}, u32[]{:S(2)}) async-start(bf16[128,4,384]{2,1,0:T(4,128)(2,1)} %get-tuple-element.55), calls=%async_computation.1 | async-start | bytes 786432 | tf_op jit(solution)/shard_map/all_to_all | solution.py:23
  39.1 1.6 subtract_convert_fusion
  40.8 1.7 pad_maximum_fusion.1.weights_ref
  42.5 8.6 %all-to-all-done.1.rows_ref = bf16[128,4,384]{2,1,0:T(4,128)(2,1)S(1)} async-done(((bf16[128,4,384]{2,1,0:T(4,128)(2,1)}), bf16[128,4,384]{2,1,0:T(4,128)(2,1)S(1)}, u32[]{:S(2)}, u32[]{:S(2)}) %all-to-all-start.1) | async-done | bytes 393248 | tf_op jit(solution)/shard_map/all_to_all | solution.py:23
  51.1 6.6 %shard_map.258 = (bf16[128,4,384]{2,1,0:T(4,128)(2,1)}, f32[2,256,384]{2,1,0:T(8,128)}, f32[2,256,384]{2,1,0:T(8,128)}) custom-call(bf16[128,4,384]{2,1,0:T(4,128)(2,1)S(1)} %all-to-all-done.1.rows_ref, bf16[2,256,256]{2,1,0:T(8,128)(2,1)} %constant.81.clone.table_ref, bf16[2,256,256]{2,1,0:T(8,128)(2,1)} %constant.82.clone.turned_ref, ...), custom_call_target="tpu_custom_call" | custom-call | tf_op jit(solution)/shard_map/pallas_call | solution.py:327
  57.7 4.1 %all-to-all-start.2 = ((bf16[128,4,384]{2,1,0:T(4,128)(2,1)}), bf16[128,4,384]{2,1,0:T(4,128)(2,1)S(1)}, u32[]{:S(2)}, u32[]{:S(2)}) async-start(bf16[128,4,384]{2,1,0:T(4,128)(2,1)} %get-tuple-element.56), calls=%async_computation.2 | async-start | bytes 786432 | tf_op jit(solution)/shard_map/all_to_all | solution.py:23
  62.7 11.7 %all-to-all-done.2.rows_ref = bf16[128,4,384]{2,1,0:T(4,128)(2,1)S(1)} async-done(((bf16[128,4,384]{2,1,0:T(4,128)(2,1)}), bf16[128,4,384]{2,1,0:T(4,128)(2,1)S(1)}, u32[]{:S(2)}, u32[]{:S(2)}) %all-to-all-start.2) | async-done | bytes 393248 | tf_op jit(solution)/shard_map/all_to_all | solution.py:23
  74.4 3.7 %shard_map.259 = (bf16[360,768]{1,0:T(8,128)(2,1)S(1)}, f32[360,768]{1,0:T(8,128)}, f32[360,128]{1,0:T(8,128)}) custom-call(bf16[128,4,384]{2,1,0:T(4,128)(2,1)S(1)} %all-to-all-done.2.rows_ref, bf16[2,360,256]{2,1,0:T(8,128)(2,1)} %constant.83.clone.table_ref, f32[360,768]{1,0:T(8,128)} %copy-done, f32[360,768]{1,0:T(8,128)} %get-tuple-element.57.xhat_ref, ...), custom_call_target="tpu_custom_call" | custom-call | tf_op jit(solution)/shard_map/pallas_call | solution.py:327
  78.1 11.0 %shard_map.260 = (bf16[360,3072]{1,0:T(8,128)(2,1)S(1)}, bf16[360,3072]{1,0:T(8,128)(2,1)S(1)}, bf16[360,3072]{1,0:T(8,128)(2,1)}, f32[8,1,384]{2,1,0:T(1,128)S(1)}) custom-call(s32[7]{0:T(128)S(1)} %stack.43.place_ref.refs_0_, bf16[360,768]{1,0:T(8,128)(2,1)S(1)} %get-tuple-element.58.flat_ref, bf16[360,768]{1,0:T(8,128)(2,1)S(1)} %reshape.270.cot_ref, ...), custom_call_target="tpu_custom_call" | custom-call | flops 3397386240 | bytes 18874368 | tf_op jit(solution)/shard_map/pallas_call | solution.py:327
  89.1 1.4 copy-done.5
  91.2 2.0 fusion.10.grad_ref
  93.2 4.3 %shard_map.261 = (bf16[128,4,384]{2,1,0:T(4,128)(2,1)}, f32[360,768]{1,0:T(8,128)}, f32[3,768]{1,0:T(4,128)}) custom-call(f32[360,768]{1,0:T(8,128)S(1)} %fusion.10.grad_ref, bf16[360,768]{1,0:T(8,128)(2,1)S(1)} %reshape.270.cot_ref, f32[360,768]{1,0:T(8,128)} %get-tuple-element.60.xhat2_ref, f32[360,128]{1,0:T(8,128)} %get-tuple-element.61.rstd2_ref, ...), custom_call_target="tpu_custom_call" | custom-call | tf_op jit(solution)/shard_map/pallas_call | solution.py:327
  98.2 3.9 %all-to-all-start.3 = ((bf16[128,4,384]{2,1,0:T(4,128)(2,1)}), bf16[128,4,384]{2,1,0:T(4,128)(2,1)S(1)}, u32[]{:S(2)}, u32[]{:S(2)}) async-start(bf16[128,4,384]{2,1,0:T(4,128)(2,1)} %get-tuple-element.62), calls=%async_computation.3 | async-start | bytes 786432 | tf_op jit(solution)/shard_map/all_to_all | solution.py:23
  102.2 1.6 copy-done.4
  103.8 1.6 copy-done.6
  105.4 14.1 %shard_map.262 = (f32[16,48,768]{2,1,0:T(8,128)}, bf16[16,48,768]{2,1,0:T(8,128)(2,1)}, bf16[16,48,768]{2,1,0:T(8,128)(2,1)}, bf16[16,48,768]{2,1,0:T(8,128)(2,1)}) custom-call(s32[7]{0:T(128)S(1)} %stack.43.place_ref.refs_0_, bf16[360,3072]{1,0:T(8,128)(2,1)S(1)} %copy-done.4, bf16[360,3072]{1,0:T(8,128)(2,1)S(1)} %copy-done.6, ...), custom_call_target="tpu_custom_call" | custom-call | flops 3397386240 | bytes 14680064 | tf_op jit(solution)/shard_map/pallas_call | solution.py:327
  119.5 10.1 %shard_map.263 = bf16[128,8,384]{2,1,0:T(8,128)(2,1)} custom-call(bf16[128,4,384]{2,1,0:T(4,128)(2,1)S(1)} %all-to-all-done.3.rows_ref, bf16[2,256,256]{2,1,0:T(8,128)(2,1)} %constant.81.clone.table_ref, bf16[2,256,256]{2,1,0:T(8,128)(2,1)} %constant.82.clone.turned_ref, bf16[2,4,384,384]{3,2,1,0:T(8,128)(2,1)} %pad_maximum_fusion.1.weights_ref, ...), custom_call_target="tpu_custom_call" | custom-call | tf_op jit(solution)/shard_map/pallas_call | solution.py:327
  129.6 9.8 %all-to-all-start.4 = ((bf16[128,8,384]{2,1,0:T(8,128)(2,1)}), bf16[128,8,384]{2,1,0:T(8,128)(2,1)S(1)}, u32[]{:S(2)}, u32[]{:S(2)}) async-start(bf16[128,8,384]{2,1,0:T(8,128)(2,1)} %shard_map.263), calls=%async_computation.4 | async-start | bytes 1572864 | tf_op jit(solution)/shard_map/all_to_all | solution.py:23
  139.5 1.4 collective-permute-start.2
  140.9 2.5 %collective-permute-start.3 = (bf16[16,48,768]{2,1,0:T(8,128)(2,1)}, bf16[16,48,768]{2,1,0:T(8,128)(2,1)}, u32[]{:S(2)}, u32[]{:S(2)}) collective-permute-start(bf16[16,48,768]{2,1,0:T(8,128)(2,1)} %get-tuple-element.66), channel_id=1, source_target_pairs={{0,2},{1,9},{2,0},{3,11},{4,6},{5,13},{6,4},{7,15},{8,10},{9,1},{1... | collective-permute-start | bytes 3538952 | tf_op jit(solution)/shard_map/ppermute | solution.py:443
  143.3 1.1 collective-permute-start.4
  144.5 11.5 %all-to-all-done.4.rows_ref = bf16[128,8,384]{2,1,0:T(8,128)(2,1)S(1)} async-done(((bf16[128,8,384]{2,1,0:T(8,128)(2,1)}), bf16[128,8,384]{2,1,0:T(8,128)(2,1)S(1)}, u32[]{:S(2)}, u32[]{:S(2)}) %all-to-all-start.4) | async-done | bytes 786464 | tf_op jit(solution)/shard_map/all_to_all | solution.py:23
  157.3 4.1 %all-to-all-start.5 = ((bf16[128,8,384]{2,1,0:T(8,128)(2,1)}), bf16[128,8,384]{2,1,0:T(8,128)(2,1)S(1)}, u32[]{:S(2)}, u32[]{:S(2)}) async-start(bf16[128,8,384]{2,1,0:T(8,128)(2,1)} %broadcast_in_dim.32), calls=%async_computation.5 | async-start | bytes 1572864 | tf_op jit(solution)/shard_map/all_to_all | solution.py:23
  161.4 2.3 %collective-permute-done.2.refs_0_ = bf16[16,48,768]{2,1,0:T(8,128)(2,1)S(1)} collective-permute-done((bf16[16,48,768]{2,1,0:T(8,128)(2,1)}, bf16[16,48,768]{2,1,0:T(8,128)(2,1)S(1)}, u32[]{:S(2)}, u32[]{:S(2)}) %collective-permute-start.2) | collective-permute-done | bytes 1179680 | tf_op jit(solution)/shard_map/ppermute | solution.py:443
  163.6 17.2 %collective-permute-done.3.refs_1_ = bf16[16,48,768]{2,1,0:T(8,128)(2,1)} collective-permute-done((bf16[16,48,768]{2,1,0:T(8,128)(2,1)}, bf16[16,48,768]{2,1,0:T(8,128)(2,1)}, u32[]{:S(2)}, u32[]{:S(2)}) %collective-permute-start.3) | collective-permute-done | bytes 1179680 | tf_op jit(solution)/shard_map/ppermute | solution.py:443
  180.9 1.7 copy-done.1
  182.5 2.1 shard_map.264
  184.7 1.4 collective-permute-start.5
  186.1 3.0 %collective-permute-start.6 = (bf16[4,48,768]{2,1,0:T(8,128)(2,1)S(1)}, bf16[4,48,768]{2,1,0:T(8,128)(2,1)S(1)}, u32[]{:S(2)}, u32[]{:S(2)}) collective-permute-start(bf16[4,48,768]{2,1,0:T(8,128)(2,1)S(1)} %get-tuple-element.75), channel_id=1, source_target_pairs={{0,8},{1,33},{2,10},{3,35},{4,12},{5,37},{6,14},{7,39},{8,0},{9,41... | collective-permute-start | bytes 884744 | tf_op jit(solution)/shard_map/ppermute | solution.py:443
  190.0 3.7 %shard_map.265 = f32[360,1,768]{2,1,0:T(1,128)} custom-call(bf16[128,8,384]{2,1,0:T(8,128)(2,1)S(1)} %all-to-all-done.4.rows_ref, bf16[2,360,256]{2,1,0:T(8,128)(2,1)} %constant.85.clone.table_ref, f32[360,768]{1,0:T(8,128)} %get-tuple-element.78.mixed_ref, f32[360,768]{1,0:T(8,128)} %get-tuple-element.57.xhat_ref, f32[360,128]{1,0:T(8,128)} %get-tuple-element.79.rstd_ref, ...), custom_call_target="tpu_custom_call" | custom-call | tf_op jit(solution)/shard_map/pallas_call | solution.py:327
  193.8 2.9 %collective-permute-done.6.refs_1_ = bf16[4,48,768]{2,1,0:T(8,128)(2,1)S(1)} collective-permute-done((bf16[4,48,768]{2,1,0:T(8,128)(2,1)S(1)}, bf16[4,48,768]{2,1,0:T(8,128)(2,1)S(1)}, u32[]{:S(2)}, u32[]{:S(2)}) %collective-permute-start.6) | collective-permute-done | bytes 294944 | tf_op jit(solution)/shard_map/ppermute | solution.py:443
  197.3 2.2 %collective-permute-start.10 = (bf16[48,768]{1,0:T(8,128)(2,1)S(1)}, bf16[48,768]{1,0:T(8,128)(2,1)S(1)}, u32[]{:S(2)}, u32[]{:S(2)}) collective-permute-start(bf16[48,768]{1,0:T(8,128)(2,1)S(1)} %get-tuple-element.85), channel_id=1, source_target_pairs={{0,48},{1,67},{2,50},{3,65},{4,52},{5,71},{6,54},{7,69},{8,56},{9,... | collective-permute-start | bytes 221192 | tf_op jit(solution)/shard_map/ppermute | solution.py:443
  199.5 1.7 collective-permute-start.9
  201.2 3.5 %collective-permute-done.8.refs_2_ = bf16[48,768]{1,0:T(8,128)(2,1)S(1)} collective-permute-done((bf16[48,768]{1,0:T(8,128)(2,1)S(1)}, bf16[48,768]{1,0:T(8,128)(2,1)S(1)}, u32[]{:S(2)}, u32[]{:S(2)}) %collective-permute-start.8) | collective-permute-done | bytes 73760 | tf_op jit(solution)/shard_map/ppermute | solution.py:443
  205.3 3.2 %collective-permute-start.11 = (f32[24,768]{1,0:T(8,128)S(1)}, f32[24,768]{1,0:T(8,128)S(1)}, u32[]{:S(2)}, u32[]{:S(2)}) collective-permute-start(f32[24,768]{1,0:T(8,128)S(1)} %get-tuple-element.87), channel_id=1, source_target_pairs={{0,1},{1,0},{2,3},{3,2},{4,5},{5,4},{6,7},{7,6},{8,9},{9,8},{10,11... | collective-permute-start | bytes 221192 | tf_op jit(solution)/shard_map/ppermute | solution.py:463
  208.5 1.9 shard_map.268
  210.4 1.3 reduce
  211.7 1.3 reduce.1
  213.0 1.3 reduce.2
  (73 shorter events, 8.0 us)
Async XLA Ops:
  0.6 15.3 %copy-start.10 = (f32[2,8,96,96]{3,2,1,0:T(8,128)S(1)}, f32[2,8,96,96]{3,2,1,0:T(8,128)}, u32[]{:S(2)}) copy-start(f32[2,8,96,96]{3,2,1,0:T(8,128)} %param.23) | copy-start | bytes 1769476
  0.7 27.2 %all-to-all-start = ((bf16[64,2,2160]{2,1,0:T(2,128)(2,1)}), bf16[64,2,2160]{2,1,0:T(2,128)(2,1)S(1)}, u32[]{:S(2)}, u32[]{:S(2)}) async-start(bf16[64,2,2160]{2,1,0:T(2,128)(2,1)} %bitcast.43), calls=%async_computation | async-start | bytes 1114112 | tf_op jit(solution)/shard_map/all_to_all | solution.py:23
  17.0 1.3 copy-start.13
  18.3 1.4 copy-start.7
  31.3 9.4 %copy-start = (f32[360,768]{1,0:T(8,128)}, f32[360,768]{1,0:T(8,128)S(1)}, u32[]{:S(2)}) copy-start(f32[360,768]{1,0:T(8,128)S(1)} %reshape.278.base_ref) | copy-start | bytes 3317764
  31.3 7.1 %copy-start.11 = (f32[2,768]{1,0:T(2,128)S(1)}, f32[2,768]{1,0:T(2,128)}, u32[]{:S(2)}) copy-start(f32[2,768]{1,0:T(2,128)} %param.22) | copy-start | bytes 18436
  31.4 7.1 %copy-start.12 = (f32[2,768]{1,0:T(2,128)S(1)}, f32[2,768]{1,0:T(2,128)}, u32[]{:S(2)}) copy-start(f32[2,768]{1,0:T(2,128)} %param.24) | copy-start | bytes 18436
  34.5 16.5 %all-to-all-start.1 = ((bf16[128,4,384]{2,1,0:T(4,128)(2,1)}), bf16[128,4,384]{2,1,0:T(4,128)(2,1)S(1)}, u32[]{:S(2)}, u32[]{:S(2)}) async-start(bf16[128,4,384]{2,1,0:T(4,128)(2,1)} %get-tuple-element.55), calls=%async_computation.1 | async-start | bytes 786432 | tf_op jit(solution)/shard_map/all_to_all | solution.py:23
  39.1 1.6 copy-start.8
  42.5 19.3 %copy-start.14 = (f32[768]{0:T(1024)S(1)}, f32[768]{0:T(1024)}, u32[]{:S(2)}) copy-start(f32[768]{0:T(1024)} %param.25) | copy-start | bytes 9220
  57.7 4.2 %copy-start.9 = (bf16[2,1,180,768]{3,0,2,1:T(2,128)(2,1)S(1)}, bf16[2,1,180,768]{3,0,2,1:T(2,128)(2,1)}, u32[]{:S(2)}) copy-start(bf16[2,1,180,768]{3,0,2,1:T(2,128)(2,1)} %param.29) | copy-start | bytes 1658884
  57.7 16.8 %all-to-all-start.2 = ((bf16[128,4,384]{2,1,0:T(4,128)(2,1)}), bf16[128,4,384]{2,1,0:T(4,128)(2,1)S(1)}, u32[]{:S(2)}, u32[]{:S(2)}) async-start(bf16[128,4,384]{2,1,0:T(4,128)(2,1)} %get-tuple-element.56), calls=%async_computation.2 | async-start | bytes 786432 | tf_op jit(solution)/shard_map/all_to_all | solution.py:23
  74.4 3.7 %copy-start.2 = (f32[3072]{0:T(1024)S(1)}, f32[3072]{0:T(1024)}, u32[]{:S(2)}) copy-start(f32[3072]{0:T(1024)} %param.27) | copy-start | bytes 36868
  78.1 13.1 %slice-start = ((s8[4718592]{0:T(1024)(128)(4,1)}), s8[4194304]{0:T(1024)(128)(4,1)S(1)}, s32[]{:S(2)}) async-start(s8[4718592]{0:T(1024)(128)(4,1)} %bitcast.45), calls=%async_computation.6 | async-start | bytes 8388608
  78.1 13.1 %slice-start.1 = ((s8[4718592]{0:T(1024)(128)(4,1)}), s8[524288]{0:T(1024)(128)(4,1)S(1)}, s32[]{:S(2)}) async-start(s8[4718592]{0:T(1024)(128)(4,1)} %bitcast.45), calls=%async_computation.7 | async-start | bytes 1048576
  89.1 1.4 copy-start.5
  90.6 2.7 %copy-start.3 = (bf16[360,3072]{1,0:T(8,128)(2,1)}, bf16[360,3072]{1,0:T(8,128)(2,1)S(1)}, u32[]{:S(2)}) copy-start(bf16[360,3072]{1,0:T(8,128)(2,1)S(1)} %get-tuple-element.59.grad_ref) | copy-start | bytes 6635524
  90.6 11.6 %collective-permute-start = (bf16[360,3072]{1,0:T(8,128)(2,1)}, bf16[360,3072]{1,0:T(8,128)(2,1)}, u32[]{:S(2)}, u32[]{:S(2)}) collective-permute-start(bf16[360,3072]{1,0:T(8,128)(2,1)} %get-tuple-element.64), channel_id=1, source_target_pairs={{0,1},{1,0},{2,3},{3,2},{4,5},{5,4},{6,7},{7,6},{8,9},{9,8},{10,11... | collective-permute-start | bytes 6635528 | tf_op jit(solution)/shard_map/ppermute | solution.py:463
  91.0 11.1 %collective-permute-start.1 = (bf16[360,768]{1,0:T(8,128)(2,1)S(1)}, bf16[360,768]{1,0:T(8,128)(2,1)S(1)}, u32[]{:S(2)}, u32[]{:S(2)}) collective-permute-start(bf16[360,768]{1,0:T(8,128)(2,1)S(1)} %broadcast_select_fusion.1), channel_id=1, source_target_pairs={{0,1},{1,0},{2,3},{3,2},{4,5},{5,4},{6,7},{7,6},{8,9},{9,8},{10,11... | collective-permute-start | bytes 1658888 | tf_op jit(solution)/shard_map/ppermute | solution.py:463
  98.2 21.3 %all-to-all-start.3 = ((bf16[128,4,384]{2,1,0:T(4,128)(2,1)}), bf16[128,4,384]{2,1,0:T(4,128)(2,1)S(1)}, u32[]{:S(2)}, u32[]{:S(2)}) async-start(bf16[128,4,384]{2,1,0:T(4,128)(2,1)} %get-tuple-element.62), calls=%async_computation.3 | async-start | bytes 786432 | tf_op jit(solution)/shard_map/all_to_all | solution.py:23
  102.2 1.6 copy-start.4
  103.8 1.6 copy-start.6
  129.6 26.3 %all-to-all-start.4 = ((bf16[128,8,384]{2,1,0:T(8,128)(2,1)}), bf16[128,8,384]{2,1,0:T(8,128)(2,1)S(1)}, u32[]{:S(2)}, u32[]{:S(2)}) async-start(bf16[128,8,384]{2,1,0:T(8,128)(2,1)} %shard_map.263), calls=%async_computation.4 | async-start | bytes 1572864 | tf_op jit(solution)/shard_map/all_to_all | solution.py:23
  139.5 24.1 %collective-permute-start.2 = (bf16[16,48,768]{2,1,0:T(8,128)(2,1)}, bf16[16,48,768]{2,1,0:T(8,128)(2,1)S(1)}, u32[]{:S(2)}, u32[]{:S(2)}) collective-permute-start(bf16[16,48,768]{2,1,0:T(8,128)(2,1)} %get-tuple-element.65), channel_id=1, source_target_pairs={{0,64},{1,5},{2,66},{3,7},{4,68},{5,9},{6,70},{7,11},{8,72},{9,13}... | collective-permute-start | bytes 3538952 | tf_op jit(solution)/shard_map/ppermute | solution.py:443
  140.9 40.0 %collective-permute-start.3 = (bf16[16,48,768]{2,1,0:T(8,128)(2,1)}, bf16[16,48,768]{2,1,0:T(8,128)(2,1)}, u32[]{:S(2)}, u32[]{:S(2)}) collective-permute-start(bf16[16,48,768]{2,1,0:T(8,128)(2,1)} %get-tuple-element.66), channel_id=1, source_target_pairs={{0,2},{1,9},{2,0},{3,11},{4,6},{5,13},{6,4},{7,15},{8,10},{9,1},{1... | collective-permute-start | bytes 3538952 | tf_op jit(solution)/shard_map/ppermute | solution.py:443
  143.3 37.5 %collective-permute-start.4 = (bf16[16,48,768]{2,1,0:T(8,128)(2,1)}, bf16[16,48,768]{2,1,0:T(8,128)(2,1)}, u32[]{:S(2)}, u32[]{:S(2)}) collective-permute-start(bf16[16,48,768]{2,1,0:T(8,128)(2,1)} %get-tuple-element.67), channel_id=1, source_target_pairs={{0,66},{1,13},{2,64},{3,15},{4,70},{5,1},{6,68},{7,3},{8,74},{9,5}... | collective-permute-start | bytes 3538952 | tf_op jit(solution)/shard_map/ppermute | solution.py:443
  157.3 51.3 %all-to-all-start.5 = ((bf16[128,8,384]{2,1,0:T(8,128)(2,1)}), bf16[128,8,384]{2,1,0:T(8,128)(2,1)S(1)}, u32[]{:S(2)}, u32[]{:S(2)}) async-start(bf16[128,8,384]{2,1,0:T(8,128)(2,1)} %broadcast_in_dim.32), calls=%async_computation.5 | async-start | bytes 1572864 | tf_op jit(solution)/shard_map/all_to_all | solution.py:23
  180.9 1.7 copy-start.1
  184.7 9.1 %collective-permute-start.5 = (bf16[4,48,768]{2,1,0:T(8,128)(2,1)S(1)}, bf16[4,48,768]{2,1,0:T(8,128)(2,1)S(1)}, u32[]{:S(2)}, u32[]{:S(2)}) collective-permute-start(bf16[4,48,768]{2,1,0:T(8,128)(2,1)S(1)} %get-tuple-element.74), channel_id=1, source_target_pairs={{0,4},{1,17},{2,6},{3,19},{4,8},{5,21},{6,10},{7,23},{8,12},{9,25}... | collective-permute-start | bytes 884744 | tf_op jit(solution)/shard_map/ppermute | solution.py:443
  186.1 10.5 %collective-permute-start.6 = (bf16[4,48,768]{2,1,0:T(8,128)(2,1)S(1)}, bf16[4,48,768]{2,1,0:T(8,128)(2,1)S(1)}, u32[]{:S(2)}, u32[]{:S(2)}) collective-permute-start(bf16[4,48,768]{2,1,0:T(8,128)(2,1)S(1)} %get-tuple-element.75), channel_id=1, source_target_pairs={{0,8},{1,33},{2,10},{3,35},{4,12},{5,37},{6,14},{7,39},{8,0},{9,41... | collective-permute-start | bytes 884744 | tf_op jit(solution)/shard_map/ppermute | solution.py:443
  189.1 7.6 %collective-permute-start.7 = (bf16[4,48,768]{2,1,0:T(8,128)(2,1)S(1)}, bf16[4,48,768]{2,1,0:T(8,128)(2,1)S(1)}, u32[]{:S(2)}, u32[]{:S(2)}) collective-permute-start(bf16[4,48,768]{2,1,0:T(8,128)(2,1)S(1)} %get-tuple-element.76), channel_id=1, source_target_pairs={{0,12},{1,49},{2,14},{3,51},{4,0},{5,53},{6,2},{7,55},{8,4},{9,57}... | collective-permute-start | bytes 884744 | tf_op jit(solution)/shard_map/ppermute | solution.py:443
  197.3 3.9 %collective-permute-start.10 = (bf16[48,768]{1,0:T(8,128)(2,1)S(1)}, bf16[48,768]{1,0:T(8,128)(2,1)S(1)}, u32[]{:S(2)}, u32[]{:S(2)}) collective-permute-start(bf16[48,768]{1,0:T(8,128)(2,1)S(1)} %get-tuple-element.85), channel_id=1, source_target_pairs={{0,48},{1,67},{2,50},{3,65},{4,52},{5,71},{6,54},{7,69},{8,56},{9,... | collective-permute-start | bytes 221192 | tf_op jit(solution)/shard_map/ppermute | solution.py:443
  199.5 5.2 %collective-permute-start.8 = (bf16[48,768]{1,0:T(8,128)(2,1)S(1)}, bf16[48,768]{1,0:T(8,128)(2,1)S(1)}, u32[]{:S(2)}, u32[]{:S(2)}) collective-permute-start(bf16[48,768]{1,0:T(8,128)(2,1)S(1)} %get-tuple-element.83), channel_id=1, source_target_pairs={{0,16},{1,65},{2,18},{3,67},{4,20},{5,69},{6,22},{7,71},{8,24},{9,... | collective-permute-start | bytes 221192 | tf_op jit(solution)/shard_map/ppermute | solution.py:443
  199.5 5.2 %collective-permute-start.9 = (bf16[48,768]{1,0:T(8,128)(2,1)S(1)}, bf16[48,768]{1,0:T(8,128)(2,1)S(1)}, u32[]{:S(2)}, u32[]{:S(2)}) collective-permute-start(bf16[48,768]{1,0:T(8,128)(2,1)S(1)} %get-tuple-element.84), channel_id=1, source_target_pairs={{0,32},{1,3},{2,34},{3,1},{4,36},{5,7},{6,38},{7,5},{8,40},{9,11},... | collective-permute-start | bytes 221192 | tf_op jit(solution)/shard_map/ppermute | solution.py:443
  205.3 8.9 %collective-permute-start.11 = (f32[24,768]{1,0:T(8,128)S(1)}, f32[24,768]{1,0:T(8,128)S(1)}, u32[]{:S(2)}, u32[]{:S(2)}) collective-permute-start(f32[24,768]{1,0:T(8,128)S(1)} %get-tuple-element.87), channel_id=1, source_target_pairs={{0,1},{1,0},{2,3},{3,2},{4,5},{5,4},{6,7},{7,6},{8,9},{9,8},{10,11... | collective-permute-start | bytes 221192 | tf_op jit(solution)/shard_map/ppermute | solution.py:463
where the time goes:
time: 216 us; the launch traced here: 215 us
  waiting for transfers between devices  65.9 us (31%)
  Pallas kernels  61.9 us (29%)
  starting transfers between devices  56.4 us (26%)
  other arithmetic  15.4 us (7%)
  local copies, waits for them, and re-layouts  12.4 us (6%)
    pallas_call x12, Pallas kernels, call(): pl.pallas_call(kernel, out_shape=[(jax.ShapeDtypeStruct if i in free_outs...  61.9 us
    all_to_all x6, waiting for transfers between devices, exchange(): return lax.all_to_all(values, axes, split_axis=0, concat_axis=0, tiled=True)  40 us
    all_to_all x6, starting transfers between devices, exchange(): return lax.all_to_all(values, axes, split_axis=0, concat_axis=0, tiled=True)  38.4 us
    ppermute x9, waiting for transfers between devices, send_all(): lax.ppermute(pieces[r], EVERY, neighbours(stage, r + 1))  25.9 us
    ppermute x9, starting transfers between devices, send_all(): lax.ppermute(pieces[r], EVERY, neighbours(stage, r + 1))  14.2 us
    unnamed x36, local copies, waits for them, and re-layouts  6.52 us
  transfers between devices with their start and end apart: 18, of which 8 were waited for; matrix products, arithmetic and copies ran while one was open for 9% of the time, Pallas kernels for 13%

commit v1 on v0

--- a/solution.py
+++ b/solution.py
@@ -308,10 +308,10 @@
     def joined(*rows):
         return jnp.concatenate([lines[r : r + 1] for r in rows], axis=1)
 
-    fc_ref[...] = joined(*range(8))
-    out_ref[...] = joined(8, 9)
-    gain1_ref[...] = joined(10, 11) + joined(14, 19)
-    gain2_ref[...] = joined(12, 13)
+    fc_ref[...] = joined(*range(8))[0]
+    out_ref[...] = joined(8, 9)[0]
+    gain1_ref[...] = (joined(10, 11) + joined(14, 19))[0]
+    gain2_ref[...] = joined(12, 13)[0]
     for i in range(2):
         b1_ref[i : i + 1] = joined(15 + i, 20 + i)
         b2_ref[i : i + 1] = joined(17 + i, 22 + i)
@@ -356,7 +356,8 @@
     wide_ref,
     own_ref,
     out1_ref,
-    out2_ref,
+    near_ref,
+    wrap_ref,
     out3_ref,
     acc_ref,
 ):
@@ -381,20 +382,34 @@
             at = (at_y * 2 + at_xh) * share
             far = jnp.where(first, at_x - x, at_y - y) & 3
             spot = jnp.where(first, at_y * 4 + at_z, at_z * 4 + at_x)
-            for r, ref in enumerate((own_ref, out1_ref, out2_ref, out3_ref)):
-
-                @pl.when(far == r)
+            upper = spot >= 8
+            for ref, here, spot in (
+                (own_ref, far == 0, spot),
+                (out1_ref, far == 1, spot),
+                (near_ref, (far == 2) & (spot < 8), spot),
+                (wrap_ref, (far == 2) & upper, spot - 8),
+                (out3_ref, far == 3, spot),
+            ):
+
+                @pl.when(here)
                 def _(ref=ref, at=at, spot=spot):
                     ref[spot] = acc_ref[at : at + share].astype(ref.dtype)
 
 
+def relay_kernel(out1_ref, out3_ref, near_ref, wrap_ref, plus_ref, minus_ref):
+    plus_ref[:8] = (out1_ref[:8].astype(f32) + near_ref[...].astype(f32)).astype(bf16)
+    plus_ref[8:] = out1_ref[8:]
+    minus_ref[:8] = out3_ref[:8]
+    minus_ref[8:] = (out3_ref[8:].astype(f32) + wrap_ref[...].astype(f32)).astype(bf16)
+
+
 def plane_kernel(place_ref, own_in_ref, *refs):
-    got, own_ref, outs = refs[:3], refs[3], refs[4:]
+    got, own_ref, outs = refs[:2], refs[2], refs[3:]
     for d in range(4):
         for i in range(4):
             at = 4 * ((place_ref[4] + d) & 3) + i
             total = own_in_ref[at]
-            for r in range(3):
+            for r in range(2):
                 total = total + got[r][at].astype(f32)
             if d == 0:
                 own_ref[i] = total
@@ -470,11 +485,12 @@
     tall = swap(tall)
     wide = swap(jnp.where(first, cot, flat))
     cube = (16, hidden // 64, width)
+    half = (8,) + cube[1:]
     ahead = pl.BlockSpec((tokens, hidden // 8), lambda g: (0, g))
     across = whole(flat.shape)
     return call(
         weight_kernel,
-        [(cube, f32)] + [(cube, bf16)] * 3,
+        [(cube, f32), (cube, bf16), (half, bf16), (half, bf16), (cube, bf16)],
         place,
         grad_hidden,
         active,
@@ -485,9 +501,9 @@
         grant=24,
         grid=(8,),
         in_specs=[SMEM, ahead, ahead, across, across, ahead, across],
-        out_specs=[whole(cube)] * 4,
+        out_specs=[whole(cube), whole(cube), whole(half), whole(half), whole(cube)],
         scratch_shapes=[pltpu.VMEM((hidden // 8, width), f32)],
-        free=range(1, 7),
+        free=(3, 4, 5, 6),
         cost_estimate=pl.CostEstimate(
             flops=4 * tokens * hidden * width, bytes_accessed=14 << 20, transcendentals=0
         ),
@@ -504,9 +520,9 @@
         own,
         *got,
         grid=(1,),
-        in_specs=[SMEM] + [whole(cube)] * 4,
+        in_specs=[SMEM] + [whole(cube)] * 3,
         out_specs=[whole(row)] * 4,
-        free=range(5),
+        free=range(4),
         free_outs=range(4),
     )
 
@@ -639,7 +655,7 @@
         ],
         out_specs=[across] * 3 + [pl.BlockSpec((1, 1, hidden // 8), lambda g: (g, 0, 0))],
         free=(1, 2, 4),
-        free_outs=(0, 1, 3),
+        free_outs=(3,),
         cost_estimate=pl.CostEstimate(
             flops=4 * tokens * hidden * width,
             bytes_accessed=18 << 20,
@@ -665,7 +681,8 @@
     own, *sent = weight_start(
         place, grad_hidden_flat, active_flat, normed_flat, upstream, tall
     )
-    first_got = send_all(sent, 0)
+    near = lax.ppermute(sent[1], EVERY, neighbours(0, 1))
+    wrap = lax.ppermute(sent[2], EVERY, neighbours(0, 3))
     got = after(got, sent)
 
     lines = jnp.concatenate((bias_sum.reshape(-1, half), sums.reshape(-1, half)))
@@ -693,6 +710,13 @@
         grant=20,
     )
     got = exchange(packet, EVERY)
+    plus, minus = call(
+        relay_kernel, [(plane, bf16) for plane in (own.shape,) * 2], sent[0], sent[3], near, wrap, free=(2, 3)
+    )
+    first_got = [
+        lax.ppermute(plus, EVERY, neighbours(0, 1)),
+        lax.ppermute(minus, EVERY, neighbours(0, 3)),
+    ]
     own, *sent = weight_second(place, own, first_got)
     second_got = send_all(sent, 1)
     (grad_input,) = call(
@@ -721,10 +745,10 @@
         [
             (whole_spec, f32),
             (whole_spec, f32),
-            ((1, hidden), f32),
-            ((1, width), f32),
-            ((1, width), f32),
-            ((1, width), f32),
+            ((hidden,), f32),
+            ((width,), f32),
+            ((width,), f32),
+            ((width,), f32),
             ((2, width), f32),
             ((2, width), f32),
         ],
@@ -737,7 +761,7 @@
         lambda *refs: point_kernel(grad_scale, *refs),
         [((hidden // ranks, width), f32)] * 2,
         place,
-        own,
+        after(own, fc_grad),
         *third_got,
         in_specs=[SMEM] + [whole(own.shape)] * 4,
         free=range(5),
@@ -751,10 +775,10 @@
         grad_input.reshape(samples, lon_cells, 1, width).transpose(0, 2, 1, 3),
         grad_one.T,
         grad_two,
-        fc_grad.reshape(hidden),
-        out_grad.reshape(width),
-        gain1.reshape(width),
-        gain2.reshape(width),
+        fc_grad,
+        out_grad,
+        gain1,
+        gain2,
         spec_one_grad,
         bias1,
         spec_two_grad,

time: 216 us -> 211 us (0.977)
  waiting for transfers between devices: 65.9 us -> 57.8 us
  starting transfers between devices: 56.4 us -> 62.8 us
  local copies, waits for them, and re-layouts: 12.4 us -> 7.71 us
  other arithmetic: 15.4 us -> 11.6 us
  Pallas kernels: 61.9 us -> 65.1 us
    ppermute x0 -> x4, waiting for transfers between devices: none -> 24.2 us  [the longest x1 15 us: local(): near = lax.ppermute(sent[1], EVERY, neighbours(0, 1))]
    ppermute x9 -> x6, waiting for transfers between devices: 25.9 us -> 4.32 us  [send_all(): lax.ppermute(pieces[r], EVERY, neighbours(stage, r + 1))]
    all_to_all x6, waiting for transfers between devices: 40 us -> 28.4 us  [exchange(): return lax.all_to_all(values, axes, split_axis=0, concat_axis=0, tiled=True)]
    ppermute x0 -> x4, starting transfers between devices: none -> 5.46 us  [the longest x1 2.5 us: local(): lax.ppermute(minus, EVERY, neighbours(0, 3))]
    unnamed x36 -> x32, local copies, waits for them, and re-layouts: 6.52 us -> 1.8 us
    pallas_call x3 -> x0, other arithmetic: 3.86 us -> none  [call(): pl.pallas_call(kernel, out_shape=[(jax.ShapeDtypeStruct if i in free_outs...]
    all_to_all x6, starting transfers between devices: 38.4 us -> 42.1 us  [exchange(): return lax.all_to_all(values, axes, split_axis=0, concat_axis=0, tiled=True)]
    pallas_call x12 -> x13, Pallas kernels: 61.9 us -> 65.1 us  [call(): pl.pallas_call(kernel, out_shape=[(jax.ShapeDtypeStruct if i in free_outs...]
  transfers between devices with their start and end apart: 18 -> 19, of which waited for: 8 -> 9; matrix products, arithmetic and copies ran while one was open for 9% -> 8% of each run, Pallas kernels for 13% -> 14%
where the time goes in v1:
time: 211 us; the launch traced here: 210 us
  Pallas kernels  65.1 us (31%)
  starting transfers between devices  62.8 us (30%)
  waiting for transfers between devices  57.8 us (27%)
  other arithmetic  11.6 us (5%)
  local copies, waits for them, and re-layouts  7.71 us (4%)
  matrix products  3.62 us (2%)
    pallas_call x13, Pallas kernels, call(): pl.pallas_call(kernel, out_shape=[(jax.ShapeDtypeStruct if i in free_outs...  65.1 us
    all_to_all x6, starting transfers between devices, exchange(): return lax.all_to_all(values, axes, split_axis=0, concat_axis=0, tiled=True)  42.1 us
    all_to_all x6, waiting for transfers between devices, exchange(): return lax.all_to_all(values, axes, split_axis=0, concat_axis=0, tiled=True)  28.4 us
    ppermute x1, waiting for transfers between devices, local(): near = lax.ppermute(sent[1], EVERY, neighbours(0, 1))  15 us
    ppermute x6, starting transfers between devices, send_all(): lax.ppermute(pieces[r], EVERY, neighbours(stage, r + 1))  12.1 us
    ppermute x1, waiting for transfers between devices, local(): lax.ppermute(plus, EVERY, neighbours(0, 1))  7.74 us
    ppermute x6, waiting for transfers between devices, send_all(): lax.ppermute(pieces[r], EVERY, neighbours(stage, r + 1))  4.32 us
  transfers between devices with their start and end apart: 19, of which 9 were waited for; matrix products, arithmetic and copies ran while one was open for 8% of the time, Pallas kernels for 14%

profile of v1, /device:TPU:1, one launch (start us, length us, event | category | flops | bytes accessed | tf_op | source)
XLA Modules:
  0.0 209.7 jit_solution(12178734474649207536)
XLA Ops:
  0.7 12.6 %all-to-all-start = ((bf16[64,2,2160]{2,1,0:T(2,128)(2,1)}), bf16[64,2,2160]{2,1,0:T(2,128)(2,1)S(1)}, u32[]{:S(2)}, u32[]{:S(2)}) async-start(bf16[64,2,2160]{2,1,0:T(2,128)(2,1)} %bitcast.42), calls=%async_computation | async-start | bytes 1114112 | tf_op jit(solution)/shard_map/all_to_all | solution.py:23
  13.3 2.7 %sort.17 = (s32[64]{0:T(128)}, s32[64]{0:T(128)S(1)}) sort(s32[64]{0:T(128)} %bitcast.46, s32[64]{0:T(128)S(1)} %iota.40), dimensions={0}, to_apply=%region_0.0 | sort | flops 384 | bytes 1024 | tf_op jit(solution)/shard_map/jit(argsort)/sort | solution.py:585
  16.0 1.1 constant_dynamic-slice_fusion
  17.1 1.3 fusion.1
  18.4 1.4 fusion
  19.8 8.1 %all-to-all-done = bf16[64,2,2160]{2,1,0:T(2,128)(2,1)S(1)} async-done(((bf16[64,2,2160]{2,1,0:T(2,128)(2,1)}), bf16[64,2,2160]{2,1,0:T(2,128)(2,1)S(1)}, u32[]{:S(2)}, u32[]{:S(2)}) %all-to-all-start) | async-done | bytes 552992 | tf_op jit(solution)/shard_map/all_to_all | solution.py:23
  27.9 1.7 gather_fusion
  30.2 1.1 reshape.262.base_ref
  31.4 3.2 %shard_map.257 = (bf16[128,4,384]{2,1,0:T(4,128)(2,1)}, f32[360,768]{1,0:T(8,128)}, f32[360,128]{1,0:T(8,128)}) custom-call(f32[360,768]{1,0:T(8,128)S(1)} %reshape.262.base_ref, bf16[2,256,360]{2,1,0:T(8,128)(2,1)} %constant.80.clone.table_ref), custom_call_target="tpu_custom_call" | custom-call | tf_op jit(solution)/shard_map/pallas_call | solution.py:327
  34.5 3.9 %all-to-all-start.1 = ((bf16[128,4,384]{2,1,0:T(4,128)(2,1)}), bf16[128,4,384]{2,1,0:T(4,128)(2,1)S(1)}, u32[]{:S(2)}, u32[]{:S(2)}) async-start(bf16[128,4,384]{2,1,0:T(4,128)(2,1)} %get-tuple-element.59), calls=%async_computation.1 | async-start | bytes 786432 | tf_op jit(solution)/shard_map/all_to_all | solution.py:23
  38.5 0.7 fusion.4.vectors_ref
  39.1 1.6 subtract_convert_fusion
  40.8 1.7 pad_maximum_fusion.1.weights_ref
  42.5 8.6 %all-to-all-done.1.rows_ref = bf16[128,4,384]{2,1,0:T(4,128)(2,1)S(1)} async-done(((bf16[128,4,384]{2,1,0:T(4,128)(2,1)}), bf16[128,4,384]{2,1,0:T(4,128)(2,1)S(1)}, u32[]{:S(2)}, u32[]{:S(2)}) %all-to-all-start.1) | async-done | bytes 393248 | tf_op jit(solution)/shard_map/all_to_all | solution.py:23
  51.1 6.6 %shard_map.258 = (bf16[128,4,384]{2,1,0:T(4,128)(2,1)}, f32[2,256,384]{2,1,0:T(8,128)}, f32[2,256,384]{2,1,0:T(8,128)}) custom-call(bf16[128,4,384]{2,1,0:T(4,128)(2,1)S(1)} %all-to-all-done.1.rows_ref, bf16[2,256,256]{2,1,0:T(8,128)(2,1)} %constant.81.clone.table_ref, bf16[2,256,256]{2,1,0:T(8,128)(2,1)} %constant.82.clone.turned_ref, ...), custom_call_target="tpu_custom_call" | custom-call | tf_op jit(solution)/shard_map/pallas_call | solution.py:327
  57.7 4.1 %all-to-all-start.2 = ((bf16[128,4,384]{2,1,0:T(4,128)(2,1)}), bf16[128,4,384]{2,1,0:T(4,128)(2,1)S(1)}, u32[]{:S(2)}, u32[]{:S(2)}) async-start(bf16[128,4,384]{2,1,0:T(4,128)(2,1)} %get-tuple-element.60), calls=%async_computation.2 | async-start | bytes 786432 | tf_op jit(solution)/shard_map/all_to_all | solution.py:23
  62.7 11.7 %all-to-all-done.2.rows_ref = bf16[128,4,384]{2,1,0:T(4,128)(2,1)S(1)} async-done(((bf16[128,4,384]{2,1,0:T(4,128)(2,1)}), bf16[128,4,384]{2,1,0:T(4,128)(2,1)S(1)}, u32[]{:S(2)}, u32[]{:S(2)}) %all-to-all-start.2) | async-done | bytes 393248 | tf_op jit(solution)/shard_map/all_to_all | solution.py:23
  74.4 3.7 %shard_map.259 = (bf16[360,768]{1,0:T(8,128)(2,1)S(1)}, f32[360,768]{1,0:T(8,128)}, f32[360,128]{1,0:T(8,128)}) custom-call(bf16[128,4,384]{2,1,0:T(4,128)(2,1)S(1)} %all-to-all-done.2.rows_ref, bf16[2,360,256]{2,1,0:T(8,128)(2,1)} %constant.83.clone.table_ref, f32[360,768]{1,0:T(8,128)} %copy-done, f32[360,768]{1,0:T(8,128)} %get-tuple-element.61.xhat_ref, ...), custom_call_target="tpu_custom_call" | custom-call | tf_op jit(solution)/shard_map/pallas_call | solution.py:327
  78.1 11.4 %shard_map.260 = (bf16[360,3072]{1,0:T(8,128)(2,1)}, bf16[360,3072]{1,0:T(8,128)(2,1)}, bf16[360,3072]{1,0:T(8,128)(2,1)}, f32[8,1,384]{2,1,0:T(1,128)S(1)}) custom-call(s32[7]{0:T(128)S(1)} %stack.43.place_ref.refs_0_, bf16[360,768]{1,0:T(8,128)(2,1)S(1)} %get-tuple-element.62.flat_ref, bf16[360,768]{1,0:T(8,128)(2,1)S(1)} %reshape.258.cot_ref, ...), custom_call_target="tpu_custom_call" | custom-call | flops 3397386240 | bytes 18874368 | tf_op jit(solution)/shard_map/pallas_call | solution.py:327
  90.2 3.6 %fusion.10.grad_ref = f32[360,768]{1,0:T(8,128)S(1)} fusion(bf16[360,3072]{1,0:T(8,128)(2,1)} %get-tuple-element.63.grad_ref, bf16[768,3072]{1,0:T(8,128)(2,1)S(1)} %bitcast.45), kind=kOutput, calls=%fused_computation.42 | convolution fusion | flops 1698693120 | bytes 8036352 | tf_op jit(solution)/shard_map/tf,df->td/dot_general | solution.py:665
  93.8 4.3 %shard_map.261 = (bf16[128,4,384]{2,1,0:T(4,128)(2,1)}, f32[360,768]{1,0:T(8,128)}, f32[3,768]{1,0:T(4,128)}) custom-call(f32[360,768]{1,0:T(8,128)S(1)} %fusion.10.grad_ref, bf16[360,768]{1,0:T(8,128)(2,1)S(1)} %reshape.258.cot_ref, f32[360,768]{1,0:T(8,128)} %get-tuple-element.64.xhat2_ref, f32[360,128]{1,0:T(8,128)} %get-tuple-element.65.rstd2_ref, ...), custom_call_target="tpu_custom_call" | custom-call | tf_op jit(solution)/shard_map/pallas_call | solution.py:327
  98.1 0.7 reshape.261
  98.9 3.9 %all-to-all-start.3 = ((bf16[128,4,384]{2,1,0:T(4,128)(2,1)}), bf16[128,4,384]{2,1,0:T(4,128)(2,1)S(1)}, u32[]{:S(2)}, u32[]{:S(2)}) async-start(bf16[128,4,384]{2,1,0:T(4,128)(2,1)} %get-tuple-element.66), calls=%async_computation.3 | async-start | bytes 786432 | tf_op jit(solution)/shard_map/all_to_all | solution.py:23
  102.8 14.1 %shard_map.262 = (f32[16,48,768]{2,1,0:T(8,128)}, bf16[16,48,768]{2,1,0:T(8,128)(2,1)}, bf16[8,48,768]{2,1,0:T(8,128)(2,1)}, bf16[8,48,768]{2,1,0:T(8,128)(2,1)}, bf16[16,48,768]{2,1,0:T(8,128)(2,1)}) custom-call(s32[7]{0:T(128)S(1)} %stack.43.place_ref.refs_0_, bf16[360,3072]{1,0:T(8,128)(2,1)} %get-tuple-element.63.grad_ref, ...), custom_call_target="tpu_custom_call" | custom-call | flops 3397386240 | bytes 14680064 | tf_op jit(solution)/shard_map/pallas_call | solution.py:327
  116.9 10.1 %shard_map.263 = bf16[128,8,384]{2,1,0:T(8,128)(2,1)} custom-call(bf16[128,4,384]{2,1,0:T(4,128)(2,1)S(1)} %all-to-all-done.3.rows_ref, bf16[2,256,256]{2,1,0:T(8,128)(2,1)} %constant.81.clone.table_ref, bf16[2,256,256]{2,1,0:T(8,128)(2,1)} %constant.82.clone.turned_ref, bf16[2,4,384,384]{3,2,1,0:T(8,128)(2,1)} %pad_maximum_fusion.1.weights_ref, ...), custom_call_target="tpu_custom_call" | custom-call | tf_op jit(solution)/shard_map/pallas_call | solution.py:327
  127.0 9.8 %all-to-all-start.4 = ((bf16[128,8,384]{2,1,0:T(8,128)(2,1)}), bf16[128,8,384]{2,1,0:T(8,128)(2,1)S(1)}, u32[]{:S(2)}, u32[]{:S(2)}) async-start(bf16[128,8,384]{2,1,0:T(8,128)(2,1)} %shard_map.263), calls=%async_computation.4 | async-start | bytes 1572864 | tf_op jit(solution)/shard_map/all_to_all | solution.py:23
  136.8 1.4 collective-permute-start.2
  138.3 1.4 collective-permute-start.3
  139.7 15.0 %collective-permute-done.2.near_ref = bf16[8,48,768]{2,1,0:T(8,128)(2,1)S(1)} collective-permute-done((bf16[8,48,768]{2,1,0:T(8,128)(2,1)S(1)}, bf16[8,48,768]{2,1,0:T(8,128)(2,1)S(1)}, u32[]{:S(2)}, u32[]{:S(2)}) %collective-permute-start.2) | collective-permute-done | bytes 589856 | tf_op jit(solution)/shard_map/ppermute | solution.py:684
  154.7 3.3 %shard_map.264 = (bf16[16,48,768]{2,1,0:T(8,128)(2,1)}, bf16[16,48,768]{2,1,0:T(8,128)(2,1)}) custom-call(bf16[16,48,768]{2,1,0:T(8,128)(2,1)} %get-tuple-element.69.out1_ref, bf16[16,48,768]{2,1,0:T(8,128)(2,1)} %get-tuple-element.72.out3_ref, bf16[8,48,768]{2,1,0:T(8,128)(2,1)S(1)} %collective-permute-done.2.near_ref, ...), custom_call_target="tpu_custom_call" | custom-call | tf_op jit(solution)/shard_map/pallas_call | solution.py:327
  158.2 2.5 %collective-permute-start.5 = (bf16[16,48,768]{2,1,0:T(8,128)(2,1)}, bf16[16,48,768]{2,1,0:T(8,128)(2,1)}, u32[]{:S(2)}, u32[]{:S(2)}) collective-permute-start(bf16[16,48,768]{2,1,0:T(8,128)(2,1)} %get-tuple-element.80), channel_id=1, source_target_pairs={{0,66},{1,13},{2,64},{3,15},{4,70},{5,1},{6,68},{7,3},{8,74},{9,5}... | collective-permute-start | bytes 3538952 | tf_op jit(solution)/shard_map/ppermute | solution.py:718
  161.1 1.0 broadcast_in_dim.32
  162.0 7.8 %all-to-all-start.5 = ((bf16[128,8,384]{2,1,0:T(8,128)(2,1)}), bf16[128,8,384]{2,1,0:T(8,128)(2,1)S(1)}, u32[]{:S(2)}, u32[]{:S(2)}) async-start(bf16[128,8,384]{2,1,0:T(8,128)(2,1)} %broadcast_in_dim.32), calls=%async_computation.5 | async-start | bytes 1572864 | tf_op jit(solution)/shard_map/all_to_all | solution.py:23
  169.8 7.7 %collective-permute-done.4.refs_0_ = bf16[16,48,768]{2,1,0:T(8,128)(2,1)S(1)} collective-permute-done((bf16[16,48,768]{2,1,0:T(8,128)(2,1)}, bf16[16,48,768]{2,1,0:T(8,128)(2,1)S(1)}, u32[]{:S(2)}, u32[]{:S(2)}) %collective-permute-start.4) | collective-permute-done | bytes 1179680 | tf_op jit(solution)/shard_map/ppermute | solution.py:717
  177.5 1.4 collective-permute-done.5.refs_1_
  178.9 1.7 copy-done.1
  180.6 1.6 shard_map.265
  182.2 0.9 collective-permute-start.6
  183.2 3.6 %collective-permute-start.7 = (bf16[4,48,768]{2,1,0:T(8,128)(2,1)S(1)}, bf16[4,48,768]{2,1,0:T(8,128)(2,1)S(1)}, u32[]{:S(2)}, u32[]{:S(2)}) collective-permute-start(bf16[4,48,768]{2,1,0:T(8,128)(2,1)S(1)} %get-tuple-element.82), channel_id=1, source_target_pairs={{0,8},{1,33},{2,10},{3,35},{4,12},{5,37},{6,14},{7,39},{8,0},{9,41... | collective-permute-start | bytes 884744 | tf_op jit(solution)/shard_map/ppermute | solution.py:458
  186.8 1.2 collective-permute-start.8
  188.0 3.7 %shard_map.266 = f32[360,1,768]{2,1,0:T(1,128)} custom-call(bf16[128,8,384]{2,1,0:T(8,128)(2,1)S(1)} %all-to-all-done.4.rows_ref, bf16[2,360,256]{2,1,0:T(8,128)(2,1)} %constant.85.clone.table_ref, f32[360,768]{1,0:T(8,128)} %get-tuple-element.85.mixed_ref, f32[360,768]{1,0:T(8,128)} %get-tuple-element.61.xhat_ref, f32[360,128]{1,0:T(8,128)} %get-tuple-element.86.rstd_ref, ...), custom_call_target="tpu_custom_call" | custom-call | tf_op jit(solution)/shard_map/pallas_call | solution.py:327
  191.7 3.0 %collective-permute-done.7.refs_1_ = bf16[4,48,768]{2,1,0:T(8,128)(2,1)S(1)} collective-permute-done((bf16[4,48,768]{2,1,0:T(8,128)(2,1)S(1)}, bf16[4,48,768]{2,1,0:T(8,128)(2,1)S(1)}, u32[]{:S(2)}, u32[]{:S(2)}) %collective-permute-start.7) | collective-permute-done | bytes 294944 | tf_op jit(solution)/shard_map/ppermute | solution.py:458
  195.4 4.9 %collective-permute-start.10 = (bf16[48,768]{1,0:T(8,128)(2,1)S(1)}, bf16[48,768]{1,0:T(8,128)(2,1)S(1)}, u32[]{:S(2)}, u32[]{:S(2)}) collective-permute-start(bf16[48,768]{1,0:T(8,128)(2,1)S(1)} %get-tuple-element.91), channel_id=1, source_target_pairs={{0,32},{1,3},{2,34},{3,1},{4,36},{5,7},{6,38},{7,5},{8,40},{9,11},... | collective-permute-start | bytes 221192 | tf_op jit(solution)/shard_map/ppermute | solution.py:458
  200.5 1.2 collective-permute-start.9
  201.7 1.9 shard_map.268
  203.6 1.4 collective-permute-done.9.refs_2_
  205.6 2.6 %collective-permute-start.12 = (f32[24,768]{1,0:T(8,128)S(1)}, f32[24,768]{1,0:T(8,128)S(1)}, u32[]{:S(2)}, u32[]{:S(2)}) collective-permute-start(f32[24,768]{1,0:T(8,128)S(1)} %get-tuple-element.97), channel_id=1, source_target_pairs={{0,1},{1,0},{2,3},{3,2},{4,5},{5,4},{6,7},{7,6},{8,9},{9,8},{10,11... | collective-permute-start | bytes 221192 | tf_op jit(solution)/shard_map/ppermute | solution.py:478
  208.1 0.9 collective-permute-done.12
  (69 shorter events, 5.1 us)
Async XLA Ops:
  0.6 15.3 %copy-start.6 = (f32[2,8,96,96]{3,2,1,0:T(8,128)S(1)}, f32[2,8,96,96]{3,2,1,0:T(8,128)}, u32[]{:S(2)}) copy-start(f32[2,8,96,96]{3,2,1,0:T(8,128)} %param.23) | copy-start | bytes 1769476
  0.7 27.2 %all-to-all-start = ((bf16[64,2,2160]{2,1,0:T(2,128)(2,1)}), bf16[64,2,2160]{2,1,0:T(2,128)(2,1)S(1)}, u32[]{:S(2)}, u32[]{:S(2)}) async-start(bf16[64,2,2160]{2,1,0:T(2,128)(2,1)} %bitcast.42), calls=%async_computation | async-start | bytes 1114112 | tf_op jit(solution)/shard_map/all_to_all | solution.py:23
  17.1 1.3 copy-start.9
  18.3 1.4 copy-start.3
  31.3 9.5 %copy-start = (f32[360,768]{1,0:T(8,128)}, f32[360,768]{1,0:T(8,128)S(1)}, u32[]{:S(2)}) copy-start(f32[360,768]{1,0:T(8,128)S(1)} %reshape.262.base_ref) | copy-start | bytes 3317764
  31.3 7.1 %copy-start.7 = (f32[2,768]{1,0:T(2,128)S(1)}, f32[2,768]{1,0:T(2,128)}, u32[]{:S(2)}) copy-start(f32[2,768]{1,0:T(2,128)} %param.22) | copy-start | bytes 18436
  31.4 7.1 %copy-start.8 = (f32[2,768]{1,0:T(2,128)S(1)}, f32[2,768]{1,0:T(2,128)}, u32[]{:S(2)}) copy-start(f32[2,768]{1,0:T(2,128)} %param.24) | copy-start | bytes 18436
  34.5 16.5 %all-to-all-start.1 = ((bf16[128,4,384]{2,1,0:T(4,128)(2,1)}), bf16[128,4,384]{2,1,0:T(4,128)(2,1)S(1)}, u32[]{:S(2)}, u32[]{:S(2)}) async-start(bf16[128,4,384]{2,1,0:T(4,128)(2,1)} %get-tuple-element.59), calls=%async_computation.1 | async-start | bytes 786432 | tf_op jit(solution)/shard_map/all_to_all | solution.py:23
  39.1 1.7 copy-start.4
  42.5 19.3 %copy-start.10 = (f32[768]{0:T(1024)S(1)}, f32[768]{0:T(1024)}, u32[]{:S(2)}) copy-start(f32[768]{0:T(1024)} %param.25) | copy-start | bytes 9220
  57.7 4.2 %copy-start.5 = (bf16[2,1,180,768]{3,0,2,1:T(2,128)(2,1)S(1)}, bf16[2,1,180,768]{3,0,2,1:T(2,128)(2,1)}, u32[]{:S(2)}) copy-start(bf16[2,1,180,768]{3,0,2,1:T(2,128)(2,1)} %param.29) | copy-start | bytes 1658884
  57.7 16.8 %all-to-all-start.2 = ((bf16[128,4,384]{2,1,0:T(4,128)(2,1)}), bf16[128,4,384]{2,1,0:T(4,128)(2,1)S(1)}, u32[]{:S(2)}, u32[]{:S(2)}) async-start(bf16[128,4,384]{2,1,0:T(4,128)(2,1)} %get-tuple-element.60), calls=%async_computation.2 | async-start | bytes 786432 | tf_op jit(solution)/shard_map/all_to_all | solution.py:23
  74.4 3.7 %copy-start.2 = (f32[3072]{0:T(1024)S(1)}, f32[3072]{0:T(1024)}, u32[]{:S(2)}) copy-start(f32[3072]{0:T(1024)} %param.27) | copy-start | bytes 36868
  78.1 12.1 %slice-start = ((s8[4718592]{0:T(1024)(128)(4,1)}), s8[4194304]{0:T(1024)(128)(4,1)S(1)}, s32[]{:S(2)}) async-start(s8[4718592]{0:T(1024)(128)(4,1)} %bitcast.44), calls=%async_computation.6 | async-start | bytes 8388608
  78.1 12.1 %slice-start.1 = ((s8[4718592]{0:T(1024)(128)(4,1)}), s8[524288]{0:T(1024)(128)(4,1)S(1)}, s32[]{:S(2)}) async-start(s8[4718592]{0:T(1024)(128)(4,1)} %bitcast.44), calls=%async_computation.7 | async-start | bytes 1048576
  89.5 13.3 %collective-permute-start = (bf16[360,3072]{1,0:T(8,128)(2,1)}, bf16[360,3072]{1,0:T(8,128)(2,1)}, u32[]{:S(2)}, u32[]{:S(2)}) collective-permute-start(bf16[360,3072]{1,0:T(8,128)(2,1)} %get-tuple-element.68), channel_id=1, source_target_pairs={{0,1},{1,0},{2,3},{3,2},{4,5},{5,4},{6,7},{7,6},{8,9},{9,8},{10,11... | collective-permute-start | bytes 6635528 | tf_op jit(solution)/shard_map/ppermute | solution.py:478
  90.0 12.8 %collective-permute-start.1 = (bf16[360,768]{1,0:T(8,128)(2,1)S(1)}, bf16[360,768]{1,0:T(8,128)(2,1)S(1)}, u32[]{:S(2)}, u32[]{:S(2)}) collective-permute-start(bf16[360,768]{1,0:T(8,128)(2,1)S(1)} %broadcast_select_fusion.1), channel_id=1, source_target_pairs={{0,1},{1,0},{2,3},{3,2},{4,5},{5,4},{6,7},{7,6},{8,9},{9,8},{10,11... | collective-permute-start | bytes 1658888 | tf_op jit(solution)/shard_map/ppermute | solution.py:478
  98.9 18.1 %all-to-all-start.3 = ((bf16[128,4,384]{2,1,0:T(4,128)(2,1)}), bf16[128,4,384]{2,1,0:T(4,128)(2,1)S(1)}, u32[]{:S(2)}, u32[]{:S(2)}) async-start(bf16[128,4,384]{2,1,0:T(4,128)(2,1)} %get-tuple-element.66), calls=%async_computation.3 | async-start | bytes 786432 | tf_op jit(solution)/shard_map/all_to_all | solution.py:23
  127.0 9.8 %copy-start.12 = (bf16[8,48,768]{2,1,0:T(8,128)(2,1)S(1)}, bf16[8,48,768]{2,1,0:T(8,128)(2,1)}, u32[]{:S(2)}) copy-start(bf16[8,48,768]{2,1,0:T(8,128)(2,1)} %get-tuple-element.70) | copy-start | bytes 1769476
  127.0 11.3 %copy-start.11 = (bf16[8,48,768]{2,1,0:T(8,128)(2,1)S(1)}, bf16[8,48,768]{2,1,0:T(8,128)(2,1)}, u32[]{:S(2)}) copy-start(bf16[8,48,768]{2,1,0:T(8,128)(2,1)} %get-tuple-element.71) | copy-start | bytes 1769476
  127.0 33.7 %all-to-all-start.4 = ((bf16[128,8,384]{2,1,0:T(8,128)(2,1)}), bf16[128,8,384]{2,1,0:T(8,128)(2,1)S(1)}, u32[]{:S(2)}, u32[]{:S(2)}) async-start(bf16[128,8,384]{2,1,0:T(8,128)(2,1)} %shard_map.263), calls=%async_computation.4 | async-start | bytes 1572864 | tf_op jit(solution)/shard_map/all_to_all | solution.py:23
  136.8 17.9 %collective-permute-start.2 = (bf16[8,48,768]{2,1,0:T(8,128)(2,1)S(1)}, bf16[8,48,768]{2,1,0:T(8,128)(2,1)S(1)}, u32[]{:S(2)}, u32[]{:S(2)}) collective-permute-start(bf16[8,48,768]{2,1,0:T(8,128)(2,1)S(1)} %copy-done.12), channel_id=1, source_target_pairs={{0,64},{1,5},{2,66},{3,7},{4,68},{5,9},{6,70},{7,11},{8,72},{9,13}... | collective-permute-start | bytes 1769480 | tf_op jit(solution)/shard_map/ppermute | solution.py:684
  138.3 16.5 %collective-permute-start.3 = (bf16[8,48,768]{2,1,0:T(8,128)(2,1)S(1)}, bf16[8,48,768]{2,1,0:T(8,128)(2,1)S(1)}, u32[]{:S(2)}, u32[]{:S(2)}) collective-permute-start(bf16[8,48,768]{2,1,0:T(8,128)(2,1)S(1)} %copy-done.11), channel_id=1, source_target_pairs={{0,66},{1,13},{2,64},{3,15},{4,70},{5,1},{6,68},{7,3},{8,74},{9,5}... | collective-permute-start | bytes 1769480 | tf_op jit(solution)/shard_map/ppermute | solution.py:685
  158.0 19.5 %collective-permute-start.4 = (bf16[16,48,768]{2,1,0:T(8,128)(2,1)}, bf16[16,48,768]{2,1,0:T(8,128)(2,1)S(1)}, u32[]{:S(2)}, u32[]{:S(2)}) collective-permute-start(bf16[16,48,768]{2,1,0:T(8,128)(2,1)} %get-tuple-element.79), channel_id=1, source_target_pairs={{0,64},{1,5},{2,66},{3,7},{4,68},{5,9},{6,70},{7,11},{8,72},{9,13}... | collective-permute-start | bytes 3538952 | tf_op jit(solution)/shard_map/ppermute | solution.py:717
  158.2 20.7 %collective-permute-start.5 = (bf16[16,48,768]{2,1,0:T(8,128)(2,1)}, bf16[16,48,768]{2,1,0:T(8,128)(2,1)}, u32[]{:S(2)}, u32[]{:S(2)}) collective-permute-start(bf16[16,48,768]{2,1,0:T(8,128)(2,1)} %get-tuple-element.80), channel_id=1, source_target_pairs={{0,66},{1,13},{2,64},{3,15},{4,70},{5,1},{6,68},{7,3},{8,74},{9,5}... | collective-permute-start | bytes 3538952 | tf_op jit(solution)/shard_map/ppermute | solution.py:718
  162.0 39.7 %all-to-all-start.5 = ((bf16[128,8,384]{2,1,0:T(8,128)(2,1)}), bf16[128,8,384]{2,1,0:T(8,128)(2,1)S(1)}, u32[]{:S(2)}, u32[]{:S(2)}) async-start(bf16[128,8,384]{2,1,0:T(8,128)(2,1)} %broadcast_in_dim.32), calls=%async_computation.5 | async-start | bytes 1572864 | tf_op jit(solution)/shard_map/all_to_all | solution.py:23
  178.9 1.7 copy-start.1
  182.2 9.5 %collective-permute-start.6 = (bf16[4,48,768]{2,1,0:T(8,128)(2,1)S(1)}, bf16[4,48,768]{2,1,0:T(8,128)(2,1)S(1)}, u32[]{:S(2)}, u32[]{:S(2)}) collective-permute-start(bf16[4,48,768]{2,1,0:T(8,128)(2,1)S(1)} %get-tuple-element.81), channel_id=1, source_target_pairs={{0,4},{1,17},{2,6},{3,19},{4,8},{5,21},{6,10},{7,23},{8,12},{9,25}... | collective-permute-start | bytes 884744 | tf_op jit(solution)/shard_map/ppermute | solution.py:458
  183.2 11.5 %collective-permute-start.7 = (bf16[4,48,768]{2,1,0:T(8,128)(2,1)S(1)}, bf16[4,48,768]{2,1,0:T(8,128)(2,1)S(1)}, u32[]{:S(2)}, u32[]{:S(2)}) collective-permute-start(bf16[4,48,768]{2,1,0:T(8,128)(2,1)S(1)} %get-tuple-element.82), channel_id=1, source_target_pairs={{0,8},{1,33},{2,10},{3,35},{4,12},{5,37},{6,14},{7,39},{8,0},{9,41... | collective-permute-start | bytes 884744 | tf_op jit(solution)/shard_map/ppermute | solution.py:458
  186.8 7.9 %collective-permute-start.8 = (bf16[4,48,768]{2,1,0:T(8,128)(2,1)S(1)}, bf16[4,48,768]{2,1,0:T(8,128)(2,1)S(1)}, u32[]{:S(2)}, u32[]{:S(2)}) collective-permute-start(bf16[4,48,768]{2,1,0:T(8,128)(2,1)S(1)} %get-tuple-element.83), channel_id=1, source_target_pairs={{0,12},{1,49},{2,14},{3,51},{4,0},{5,53},{6,2},{7,55},{8,4},{9,57}... | collective-permute-start | bytes 884744 | tf_op jit(solution)/shard_map/ppermute | solution.py:458
  195.4 8.2 %collective-permute-start.10 = (bf16[48,768]{1,0:T(8,128)(2,1)S(1)}, bf16[48,768]{1,0:T(8,128)(2,1)S(1)}, u32[]{:S(2)}, u32[]{:S(2)}) collective-permute-start(bf16[48,768]{1,0:T(8,128)(2,1)S(1)} %get-tuple-element.91), channel_id=1, source_target_pairs={{0,32},{1,3},{2,34},{3,1},{4,36},{5,7},{6,38},{7,5},{8,40},{9,11},... | collective-permute-start | bytes 221192 | tf_op jit(solution)/shard_map/ppermute | solution.py:458
  200.3 3.3 %collective-permute-start.11 = (bf16[48,768]{1,0:T(8,128)(2,1)S(1)}, bf16[48,768]{1,0:T(8,128)(2,1)S(1)}, u32[]{:S(2)}, u32[]{:S(2)}) collective-permute-start(bf16[48,768]{1,0:T(8,128)(2,1)S(1)} %get-tuple-element.92), channel_id=1, source_target_pairs={{0,48},{1,67},{2,50},{3,65},{4,52},{5,71},{6,54},{7,69},{8,56},{9,... | collective-permute-start | bytes 221192 | tf_op jit(solution)/shard_map/ppermute | solution.py:458
  200.5 4.4 %collective-permute-start.9 = (bf16[48,768]{1,0:T(8,128)(2,1)S(1)}, bf16[48,768]{1,0:T(8,128)(2,1)S(1)}, u32[]{:S(2)}, u32[]{:S(2)}) collective-permute-start(bf16[48,768]{1,0:T(8,128)(2,1)S(1)} %get-tuple-element.90), channel_id=1, source_target_pairs={{0,16},{1,65},{2,18},{3,67},{4,20},{5,69},{6,22},{7,71},{8,24},{9,... | collective-permute-start | bytes 221192 | tf_op jit(solution)/shard_map/ppermute | solution.py:458
  205.6 3.5 %collective-permute-start.12 = (f32[24,768]{1,0:T(8,128)S(1)}, f32[24,768]{1,0:T(8,128)S(1)}, u32[]{:S(2)}, u32[]{:S(2)}) collective-permute-start(f32[24,768]{1,0:T(8,128)S(1)} %get-tuple-element.97), channel_id=1, source_target_pairs={{0,1},{1,0},{2,3},{3,2},{4,5},{5,4},{6,7},{7,6},{8,9},{9,8},{10,11... | collective-permute-start | bytes 221192 | tf_op jit(solution)/shard_map/ppermute | solution.py:478

commit v2 on v1

--- a/solution.py
+++ b/solution.py
@@ -170,19 +170,20 @@
 
 
 def mix(real, imag, weights, index):
-    wr = (weights[0, index], weights[1, index])
-    wi = (weights[0, index + 1], weights[1, index + 1])
-    real, imag = split(real), split(imag)
-    return dot3(real, wr) - dot3(imag, wi), dot3(real, wi) + dot3(imag, wr)
+    both = (weights[0, index], weights[1, index])
+    first, second = dot3(split(real), both), dot3(split(imag), both)
+    n = first.shape[1] // 2
+    return first[:, :n] - second[:, n:], first[:, n:] + second[:, :n]
+
+
+def beside(left, right):
+    return tuple(jnp.concatenate(pair, axis=1) for pair in zip(left, right))
 
 
 def mix_pull(real, imag, weights, index):
-    wr = (weights[0, index], weights[1, index])
-    wi = (weights[0, index + 1], weights[1, index + 1])
-    return (
-        dot3(real, wr, 1, 1) + dot3(imag, wi, 1, 1),
-        dot3(imag, wr, 1, 1) - dot3(real, wi, 1, 1),
-    )
+    both = (weights[0, index], weights[1, index])
+    turned = beside(imag, tuple(-r for r in real))
+    return dot3(beside(real, imag), both, 1, 1), dot3(turned, both, 1, 1)
 
 
 def compact(full, inner):
@@ -209,7 +210,7 @@
     imag = imag + vectors_ref[2:3]
     pre_ref[0] = real
     pre_ref[1] = imag
-    real, imag = mix(smooth_gate(real), smooth_gate(imag), weights_ref, 2)
+    real, imag = mix(smooth_gate(real), smooth_gate(imag), weights_ref, 1)
     real = real + vectors_ref[3:4]
     imag = imag + vectors_ref[4:5]
     turned = (turned_ref[0], turned_ref[1])
@@ -246,19 +247,18 @@
     imag = jnp.concatenate((found[0][half:], found[1][half:]), axis=0)
 
     def weight_grads(first, second, grad_real, grad_imag, at):
-        grads_ref[inner * at : inner * (at + 1)] = compact(
-            dot3(first, grad_real, 0, 0) + dot3(second, grad_imag, 0, 0), inner
-        )
-        grads_ref[inner * (at + 1) : inner * (at + 2)] = compact(
-            dot3(first, grad_imag, 0, 0) - dot3(second, grad_real, 0, 0), inner
-        )
+        both = beside(grad_real, grad_imag)
+        a, b = dot3(first, both, 0, 0), dot3(second, both, 0, 0)
+        n = a.shape[1] // 2
+        grads_ref[inner * at : inner * (at + 1)] = compact(a[:, :n] + b[:, n:], inner)
+        grads_ref[inner * (at + 1) : inner * (at + 2)] = compact(a[:, n:] - b[:, :n], inner)
 
     sums_ref[3:4] = jnp.sum(real, axis=0, keepdims=True)
     sums_ref[4:5] = jnp.sum(imag, axis=0, keepdims=True)
     pre_real, pre_imag = pre_ref[0], pre_ref[1]
     real, imag = split(real), split(imag)
     weight_grads(split(smooth_gate(pre_real)), split(smooth_gate(pre_imag)), real, imag, 2)
-    real, imag = mix_pull(real, imag, weights_ref, 2)
+    real, imag = mix_pull(real, imag, weights_ref, 1)
     real = real * gate_slope(pre_real)
     imag = imag * gate_slope(pre_imag)
     sums_ref[1:2] = jnp.sum(real, axis=0, keepdims=True)
@@ -522,7 +522,7 @@
         grid=(1,),
         in_specs=[SMEM] + [whole(cube)] * 3,
         out_specs=[whole(row)] * 4,
-        free=range(4),
+        free=(2, 3),
         free_outs=range(4),
     )
 
@@ -591,12 +591,11 @@
     which = lax.axis_index("dp")
     blocks, inner = spec_one.shape[1:3]
     mine = blocks // 2
-    both = jnp.concatenate(
-        [
-            block_diagonal(lax.dynamic_slice_in_dim(w, which * mine, mine, 1))
-            for w in (spec_one, spec_two)
-        ]
-    )
+    wide = [
+        block_diagonal(lax.dynamic_slice_in_dim(w, which * mine, mine, 1))
+        for w in (spec_one, spec_two)
+    ]
+    both = jnp.stack([jnp.concatenate((w[0], w[1]), axis=1) for w in wide])
     weights = jnp.stack(split(both))
     vectors = lax.dynamic_slice_in_dim(
         jnp.concatenate((gain_one[None], bias_one, bias_two)), which * half, half, 1

time: 211 us -> 211 us (level)
  no operation moved by 1% of the time
where the time goes in v2:
time: 211 us; the launch traced here: 210 us
  Pallas kernels  65.7 us (31%)
  starting transfers between devices  62.6 us (30%)
  waiting for transfers between devices  57.3 us (27%)
  other arithmetic  11 us (5%)
  local copies, waits for them, and re-layouts  8.42 us (4%)
  matrix products  3.62 us (2%)
    pallas_call x13, Pallas kernels, call(): pl.pallas_call(kernel, out_shape=[(jax.ShapeDtypeStruct if i in free_outs...  65.7 us
    all_to_all x6, starting transfers between devices, exchange(): return lax.all_to_all(values, axes, split_axis=0, concat_axis=0, tiled=True)  42.3 us
    all_to_all x6, waiting for transfers between devices, exchange(): return lax.all_to_all(values, axes, split_axis=0, concat_axis=0, tiled=True)  27.6 us
    ppermute x1, waiting for transfers between devices, local(): near = lax.ppermute(sent[1], EVERY, neighbours(0, 1))  15 us
    ppermute x6, starting transfers between devices, send_all(): lax.ppermute(pieces[r], EVERY, neighbours(stage, r + 1))  11.7 us
    ppermute x1, waiting for transfers between devices, local(): lax.ppermute(plus, EVERY, neighbours(0, 1))  7.75 us
    ppermute x6, waiting for transfers between devices, send_all(): lax.ppermute(pieces[r], EVERY, neighbours(stage, r + 1))  4.71 us
  transfers between devices with their start and end apart: 19, of which 9 were waited for; matrix products, arithmetic and copies ran while one was open for 8% of the time, Pallas kernels for 14%

profile of v2, /device:TPU:1, one launch (start us, length us, event | category | flops | bytes accessed | tf_op | source)
XLA Modules:
  0.0 209.8 jit_solution(14510959583324159957)
XLA Ops:
  0.7 12.8 %all-to-all-start = ((bf16[64,2,2160]{2,1,0:T(2,128)(2,1)}), bf16[64,2,2160]{2,1,0:T(2,128)(2,1)}, u32[]{:S(2)}, u32[]{:S(2)}) async-start(bf16[64,2,2160]{2,1,0:T(2,128)(2,1)} %bitcast.50), calls=%async_computation | async-start | bytes 1114112 | tf_op jit(solution)/shard_map/all_to_all | solution.py:23
  13.5 1.1 constant_dynamic-slice_fusion
  14.6 1.3 maximum_select_fusion
  16.6 2.0 sort.17
  19.4 1.4 fusion
  20.8 7.2 %all-to-all-done = bf16[64,2,2160]{2,1,0:T(2,128)(2,1)} async-done(((bf16[64,2,2160]{2,1,0:T(2,128)(2,1)}), bf16[64,2,2160]{2,1,0:T(2,128)(2,1)}, u32[]{:S(2)}, u32[]{:S(2)}) %all-to-all-start) | async-done | bytes 552992 | tf_op jit(solution)/shard_map/all_to_all | solution.py:23
  28.0 2.8 %gather_fusion = bf16[64,2,2160]{2,1,0:T(2,128)(2,1)S(1)} fusion(bf16[64,2,2160]{2,1,0:T(2,128)(2,1)} %all-to-all-done, s32[1024]{0:T(1024)S(1)} %pad_clamp_fusion), kind=kCustom, calls=%fused_computation | custom fusion | bytes 1106176 | tf_op jit(solution)/shard_map/jit(_take)/gather | solution.py:586
  31.4 1.1 reshape.158.base_ref
  32.5 3.2 %shard_map.257 = (bf16[128,4,384]{2,1,0:T(4,128)(2,1)}, f32[360,768]{1,0:T(8,128)}, f32[360,128]{1,0:T(8,128)}) custom-call(f32[360,768]{1,0:T(8,128)S(1)} %reshape.158.base_ref, bf16[2,256,360]{2,1,0:T(8,128)(2,1)} %constant.80.clone.table_ref), custom_call_target="tpu_custom_call" | custom-call | tf_op jit(solution)/shard_map/pallas_call | solution.py:327
  35.7 3.9 %all-to-all-start.1 = ((bf16[128,4,384]{2,1,0:T(4,128)(2,1)}), bf16[128,4,384]{2,1,0:T(4,128)(2,1)S(1)}, u32[]{:S(2)}, u32[]{:S(2)}) async-start(bf16[128,4,384]{2,1,0:T(4,128)(2,1)} %get-tuple-element.59), calls=%async_computation.1 | async-start | bytes 786432 | tf_op jit(solution)/shard_map/all_to_all | solution.py:23
  39.6 0.7 fusion.2.vectors_ref
  40.3 1.6 subtract_convert_fusion
  41.9 1.6 pad_maximum_fusion.1.weights_ref
  43.6 8.7 %all-to-all-done.1.rows_ref = bf16[128,4,384]{2,1,0:T(4,128)(2,1)S(1)} async-done(((bf16[128,4,384]{2,1,0:T(4,128)(2,1)}), bf16[128,4,384]{2,1,0:T(4,128)(2,1)S(1)}, u32[]{:S(2)}, u32[]{:S(2)}) %all-to-all-start.1) | async-done | bytes 393248 | tf_op jit(solution)/shard_map/all_to_all | solution.py:23
  52.2 7.0 %shard_map.258 = (bf16[128,4,384]{2,1,0:T(4,128)(2,1)}, f32[2,256,384]{2,1,0:T(8,128)}, f32[2,256,384]{2,1,0:T(8,128)}) custom-call(bf16[128,4,384]{2,1,0:T(4,128)(2,1)S(1)} %all-to-all-done.1.rows_ref, bf16[2,256,256]{2,1,0:T(8,128)(2,1)} %constant.81.clone.table_ref, bf16[2,256,256]{2,1,0:T(8,128)(2,1)} %constant.82.clone.turned_ref, ...), custom_call_target="tpu_custom_call" | custom-call | tf_op jit(solution)/shard_map/pallas_call | solution.py:327
  59.2 4.1 %all-to-all-start.2 = ((bf16[128,4,384]{2,1,0:T(4,128)(2,1)}), bf16[128,4,384]{2,1,0:T(4,128)(2,1)S(1)}, u32[]{:S(2)}, u32[]{:S(2)}) async-start(bf16[128,4,384]{2,1,0:T(4,128)(2,1)} %get-tuple-element.60), calls=%async_computation.2 | async-start | bytes 786432 | tf_op jit(solution)/shard_map/all_to_all | solution.py:23
  64.3 11.7 %all-to-all-done.2.rows_ref = bf16[128,4,384]{2,1,0:T(4,128)(2,1)S(1)} async-done(((bf16[128,4,384]{2,1,0:T(4,128)(2,1)}), bf16[128,4,384]{2,1,0:T(4,128)(2,1)S(1)}, u32[]{:S(2)}, u32[]{:S(2)}) %all-to-all-start.2) | async-done | bytes 393248 | tf_op jit(solution)/shard_map/all_to_all | solution.py:23
  76.0 3.7 %shard_map.259 = (bf16[360,768]{1,0:T(8,128)(2,1)S(1)}, f32[360,768]{1,0:T(8,128)}, f32[360,128]{1,0:T(8,128)}) custom-call(bf16[128,4,384]{2,1,0:T(4,128)(2,1)S(1)} %all-to-all-done.2.rows_ref, bf16[2,360,256]{2,1,0:T(8,128)(2,1)} %constant.83.clone.table_ref, f32[360,768]{1,0:T(8,128)} %copy-done, f32[360,768]{1,0:T(8,128)} %get-tuple-element.61.xhat_ref, ...), custom_call_target="tpu_custom_call" | custom-call | tf_op jit(solution)/shard_map/pallas_call | solution.py:327
  79.7 11.4 %shard_map.260 = (bf16[360,3072]{1,0:T(8,128)(2,1)}, bf16[360,3072]{1,0:T(8,128)(2,1)}, bf16[360,3072]{1,0:T(8,128)(2,1)}, f32[8,1,384]{2,1,0:T(1,128)S(1)}) custom-call(s32[7]{0:T(128)S(1)} %stack.52.place_ref.refs_0_, bf16[360,768]{1,0:T(8,128)(2,1)S(1)} %get-tuple-element.62.flat_ref, bf16[360,768]{1,0:T(8,128)(2,1)S(1)} %reshape.154.cot_ref, ...), custom_call_target="tpu_custom_call" | custom-call | flops 3397386240 | bytes 18874368 | tf_op jit(solution)/shard_map/pallas_call | solution.py:327
  91.7 3.6 %fusion.8.grad_ref = f32[360,768]{1,0:T(8,128)S(1)} fusion(bf16[360,3072]{1,0:T(8,128)(2,1)} %get-tuple-element.63.grad_ref, bf16[768,3072]{1,0:T(8,128)(2,1)S(1)} %bitcast.53), kind=kOutput, calls=%fused_computation.46 | convolution fusion | flops 1698693120 | bytes 8036352 | tf_op jit(solution)/shard_map/tf,df->td/dot_general | solution.py:664
  95.4 4.3 %shard_map.261 = (bf16[128,4,384]{2,1,0:T(4,128)(2,1)}, f32[360,768]{1,0:T(8,128)}, f32[3,768]{1,0:T(4,128)}) custom-call(f32[360,768]{1,0:T(8,128)S(1)} %fusion.8.grad_ref, bf16[360,768]{1,0:T(8,128)(2,1)S(1)} %reshape.154.cot_ref, f32[360,768]{1,0:T(8,128)} %get-tuple-element.64.xhat2_ref, f32[360,128]{1,0:T(8,128)} %get-tuple-element.65.rstd2_ref, ...), custom_call_target="tpu_custom_call" | custom-call | tf_op jit(solution)/shard_map/pallas_call | solution.py:327
  99.7 0.7 reshape.157
  100.4 3.9 %all-to-all-start.3 = ((bf16[128,4,384]{2,1,0:T(4,128)(2,1)}), bf16[128,4,384]{2,1,0:T(4,128)(2,1)S(1)}, u32[]{:S(2)}, u32[]{:S(2)}) async-start(bf16[128,4,384]{2,1,0:T(4,128)(2,1)} %get-tuple-element.66), calls=%async_computation.3 | async-start | bytes 786432 | tf_op jit(solution)/shard_map/all_to_all | solution.py:23
  104.4 14.1 %shard_map.262 = (f32[16,48,768]{2,1,0:T(8,128)}, bf16[16,48,768]{2,1,0:T(8,128)(2,1)}, bf16[8,48,768]{2,1,0:T(8,128)(2,1)}, bf16[8,48,768]{2,1,0:T(8,128)(2,1)}, bf16[16,48,768]{2,1,0:T(8,128)(2,1)}) custom-call(s32[7]{0:T(128)S(1)} %stack.52.place_ref.refs_0_, bf16[360,3072]{1,0:T(8,128)(2,1)} %get-tuple-element.63.grad_ref, ...), custom_call_target="tpu_custom_call" | custom-call | flops 3397386240 | bytes 14680064 | tf_op jit(solution)/shard_map/pallas_call | solution.py:327
  118.5 9.5 %shard_map.263 = bf16[128,8,384]{2,1,0:T(8,128)(2,1)} custom-call(bf16[128,4,384]{2,1,0:T(4,128)(2,1)S(1)} %all-to-all-done.3.rows_ref, bf16[2,256,256]{2,1,0:T(8,128)(2,1)} %constant.81.clone.table_ref, bf16[2,256,256]{2,1,0:T(8,128)(2,1)} %constant.82.clone.turned_ref, bf16[2,2,384,768]{3,2,1,0:T(8,128)(2,1)} %pad_maximum_fusion.1.weights_ref, ...), custom_call_target="tpu_custom_call" | custom-call | tf_op jit(solution)/shard_map/pallas_call | solution.py:327
  128.0 9.8 %all-to-all-start.4 = ((bf16[128,8,384]{2,1,0:T(8,128)(2,1)}), bf16[128,8,384]{2,1,0:T(8,128)(2,1)S(1)}, u32[]{:S(2)}, u32[]{:S(2)}) async-start(bf16[128,8,384]{2,1,0:T(8,128)(2,1)} %shard_map.263), calls=%async_computation.4 | async-start | bytes 1572864 | tf_op jit(solution)/shard_map/all_to_all | solution.py:23
  137.8 1.4 collective-permute-start.2
  139.3 1.4 collective-permute-start.3
  140.7 15.0 %collective-permute-done.2.near_ref = bf16[8,48,768]{2,1,0:T(8,128)(2,1)S(1)} collective-permute-done((bf16[8,48,768]{2,1,0:T(8,128)(2,1)S(1)}, bf16[8,48,768]{2,1,0:T(8,128)(2,1)S(1)}, u32[]{:S(2)}, u32[]{:S(2)}) %collective-permute-start.2) | collective-permute-done | bytes 589856 | tf_op jit(solution)/shard_map/ppermute | solution.py:683
  155.7 3.3 %shard_map.264 = (bf16[16,48,768]{2,1,0:T(8,128)(2,1)}, bf16[16,48,768]{2,1,0:T(8,128)(2,1)}) custom-call(bf16[16,48,768]{2,1,0:T(8,128)(2,1)} %get-tuple-element.69.out1_ref, bf16[16,48,768]{2,1,0:T(8,128)(2,1)} %get-tuple-element.72.out3_ref, bf16[8,48,768]{2,1,0:T(8,128)(2,1)S(1)} %collective-permute-done.2.near_ref, ...), custom_call_target="tpu_custom_call" | custom-call | tf_op jit(solution)/shard_map/pallas_call | solution.py:327
  159.2 2.5 %collective-permute-start.5 = (bf16[16,48,768]{2,1,0:T(8,128)(2,1)}, bf16[16,48,768]{2,1,0:T(8,128)(2,1)}, u32[]{:S(2)}, u32[]{:S(2)}) collective-permute-start(bf16[16,48,768]{2,1,0:T(8,128)(2,1)} %get-tuple-element.80), channel_id=1, source_target_pairs={{0,66},{1,13},{2,64},{3,15},{4,70},{5,1},{6,68},{7,3},{8,74},{9,5}... | collective-permute-start | bytes 3538952 | tf_op jit(solution)/shard_map/ppermute | solution.py:717
  162.1 1.0 broadcast_in_dim.32
  163.0 7.8 %all-to-all-start.5 = ((bf16[128,8,384]{2,1,0:T(8,128)(2,1)}), bf16[128,8,384]{2,1,0:T(8,128)(2,1)S(1)}, u32[]{:S(2)}, u32[]{:S(2)}) async-start(bf16[128,8,384]{2,1,0:T(8,128)(2,1)} %broadcast_in_dim.32), calls=%async_computation.5 | async-start | bytes 1572864 | tf_op jit(solution)/shard_map/all_to_all | solution.py:23
  170.8 7.7 %collective-permute-done.4.refs_0_ = bf16[16,48,768]{2,1,0:T(8,128)(2,1)S(1)} collective-permute-done((bf16[16,48,768]{2,1,0:T(8,128)(2,1)}, bf16[16,48,768]{2,1,0:T(8,128)(2,1)S(1)}, u32[]{:S(2)}, u32[]{:S(2)}) %collective-permute-start.4) | collective-permute-done | bytes 1179680 | tf_op jit(solution)/shard_map/ppermute | solution.py:716
  178.5 1.4 collective-permute-done.5.refs_1_
  179.9 2.3 %shard_map.265 = (f32[4,48,768]{2,1,0:T(8,128)S(1)}, bf16[4,48,768]{2,1,0:T(8,128)(2,1)S(1)}, bf16[4,48,768]{2,1,0:T(8,128)(2,1)S(1)}, bf16[4,48,768]{2,1,0:T(8,128)(2,1)S(1)}) custom-call(s32[7]{0:T(128)S(1)} %stack.52.place_ref.refs_0_, f32[16,48,768]{2,1,0:T(8,128)} %get-tuple-element.78.own_in_ref, ...), custom_call_target="tpu_custom_call" | custom-call | tf_op jit(solution)/shard_map/pallas_call | solution.py:327
  182.3 0.9 collective-permute-start.6
  183.2 3.6 %collective-permute-start.7 = (bf16[4,48,768]{2,1,0:T(8,128)(2,1)S(1)}, bf16[4,48,768]{2,1,0:T(8,128)(2,1)S(1)}, u32[]{:S(2)}, u32[]{:S(2)}) collective-permute-start(bf16[4,48,768]{2,1,0:T(8,128)(2,1)S(1)} %get-tuple-element.82), channel_id=1, source_target_pairs={{0,8},{1,33},{2,10},{3,35},{4,12},{5,37},{6,14},{7,39},{8,0},{9,41... | collective-permute-start | bytes 884744 | tf_op jit(solution)/shard_map/ppermute | solution.py:458
  186.8 1.2 collective-permute-start.8
  188.0 3.7 %shard_map.266 = f32[360,1,768]{2,1,0:T(1,128)} custom-call(bf16[128,8,384]{2,1,0:T(8,128)(2,1)S(1)} %all-to-all-done.4.rows_ref, bf16[2,360,256]{2,1,0:T(8,128)(2,1)} %constant.85.clone.table_ref, f32[360,768]{1,0:T(8,128)} %get-tuple-element.85.mixed_ref, f32[360,768]{1,0:T(8,128)} %get-tuple-element.61.xhat_ref, f32[360,128]{1,0:T(8,128)} %get-tuple-element.86.rstd_ref, ...), custom_call_target="tpu_custom_call" | custom-call | tf_op jit(solution)/shard_map/pallas_call | solution.py:327
  191.7 3.3 %collective-permute-done.7.refs_1_ = bf16[4,48,768]{2,1,0:T(8,128)(2,1)S(1)} collective-permute-done((bf16[4,48,768]{2,1,0:T(8,128)(2,1)S(1)}, bf16[4,48,768]{2,1,0:T(8,128)(2,1)S(1)}, u32[]{:S(2)}, u32[]{:S(2)}) %collective-permute-start.7) | collective-permute-done | bytes 294944 | tf_op jit(solution)/shard_map/ppermute | solution.py:458
  195.1 0.7 shard_map.267
  195.8 4.5 %collective-permute-start.10 = (bf16[48,768]{1,0:T(8,128)(2,1)S(1)}, bf16[48,768]{1,0:T(8,128)(2,1)S(1)}, u32[]{:S(2)}, u32[]{:S(2)}) collective-permute-start(bf16[48,768]{1,0:T(8,128)(2,1)S(1)} %get-tuple-element.91), channel_id=1, source_target_pairs={{0,32},{1,3},{2,34},{3,1},{4,36},{5,7},{6,38},{7,5},{8,40},{9,11},... | collective-permute-start | bytes 221192 | tf_op jit(solution)/shard_map/ppermute | solution.py:458
  200.6 1.2 collective-permute-start.9
  201.8 1.9 shard_map.268
  203.6 1.4 collective-permute-done.9.refs_2_
  205.6 2.6 %collective-permute-start.12 = (f32[24,768]{1,0:T(8,128)S(1)}, f32[24,768]{1,0:T(8,128)S(1)}, u32[]{:S(2)}, u32[]{:S(2)}) collective-permute-start(f32[24,768]{1,0:T(8,128)S(1)} %get-tuple-element.97), channel_id=1, source_target_pairs={{0,1},{1,0},{2,3},{3,2},{4,5},{5,4},{6,7},{7,6},{8,9},{9,8},{10,11... | collective-permute-start | bytes 221192 | tf_op jit(solution)/shard_map/ppermute | solution.py:478
  208.2 0.9 collective-permute-done.12
  (73 shorter events, 5.9 us)
Async XLA Ops:
  0.6 12.8 %copy-start.5 = (f32[2,8,96,96]{3,2,1,0:T(8,128)S(1)}, f32[2,8,96,96]{3,2,1,0:T(8,128)}, u32[]{:S(2)}) copy-start(f32[2,8,96,96]{3,2,1,0:T(8,128)} %param.23) | copy-start | bytes 1769476
  0.7 27.3 %all-to-all-start = ((bf16[64,2,2160]{2,1,0:T(2,128)(2,1)}), bf16[64,2,2160]{2,1,0:T(2,128)(2,1)}, u32[]{:S(2)}, u32[]{:S(2)}) async-start(bf16[64,2,2160]{2,1,0:T(2,128)(2,1)} %bitcast.50), calls=%async_computation | async-start | bytes 1114112 | tf_op jit(solution)/shard_map/all_to_all | solution.py:23
  15.9 0.7 copy-start.12
  18.6 0.7 copy-start.8
  19.4 1.4 copy-start.2
  32.5 9.4 %copy-start = (f32[360,768]{1,0:T(8,128)}, f32[360,768]{1,0:T(8,128)S(1)}, u32[]{:S(2)}) copy-start(f32[360,768]{1,0:T(8,128)S(1)} %reshape.158.base_ref) | copy-start | bytes 3317764
  32.5 7.1 %copy-start.6 = (f32[2,768]{1,0:T(2,128)S(1)}, f32[2,768]{1,0:T(2,128)}, u32[]{:S(2)}) copy-start(f32[2,768]{1,0:T(2,128)} %param.22) | copy-start | bytes 18436
  32.5 7.1 %copy-start.7 = (f32[2,768]{1,0:T(2,128)S(1)}, f32[2,768]{1,0:T(2,128)}, u32[]{:S(2)}) copy-start(f32[2,768]{1,0:T(2,128)} %param.24) | copy-start | bytes 18436
  35.7 16.5 %all-to-all-start.1 = ((bf16[128,4,384]{2,1,0:T(4,128)(2,1)}), bf16[128,4,384]{2,1,0:T(4,128)(2,1)S(1)}, u32[]{:S(2)}, u32[]{:S(2)}) async-start(bf16[128,4,384]{2,1,0:T(4,128)(2,1)} %get-tuple-element.59), calls=%async_computation.1 | async-start | bytes 786432 | tf_op jit(solution)/shard_map/all_to_all | solution.py:23
  40.3 1.6 copy-start.3
  43.6 19.8 %copy-start.9 = (f32[768]{0:T(1024)S(1)}, f32[768]{0:T(1024)}, u32[]{:S(2)}) copy-start(f32[768]{0:T(1024)} %param.25) | copy-start | bytes 9220
  59.2 4.2 %copy-start.4 = (bf16[2,1,180,768]{3,0,2,1:T(2,128)(2,1)S(1)}, bf16[2,1,180,768]{3,0,2,1:T(2,128)(2,1)}, u32[]{:S(2)}) copy-start(bf16[2,1,180,768]{3,0,2,1:T(2,128)(2,1)} %param.29) | copy-start | bytes 1658884
  59.2 16.8 %all-to-all-start.2 = ((bf16[128,4,384]{2,1,0:T(4,128)(2,1)}), bf16[128,4,384]{2,1,0:T(4,128)(2,1)S(1)}, u32[]{:S(2)}, u32[]{:S(2)}) async-start(bf16[128,4,384]{2,1,0:T(4,128)(2,1)} %get-tuple-element.60), calls=%async_computation.2 | async-start | bytes 786432 | tf_op jit(solution)/shard_map/all_to_all | solution.py:23
  76.0 3.7 %copy-start.1 = (f32[3072]{0:T(1024)S(1)}, f32[3072]{0:T(1024)}, u32[]{:S(2)}) copy-start(f32[3072]{0:T(1024)} %param.27) | copy-start | bytes 36868
  79.7 12.1 %slice-start = ((s8[4718592]{0:T(1024)(128)(4,1)}), s8[4194304]{0:T(1024)(128)(4,1)S(1)}, s32[]{:S(2)}) async-start(s8[4718592]{0:T(1024)(128)(4,1)} %bitcast.52), calls=%async_computation.6 | async-start | bytes 8388608
  79.7 12.1 %slice-start.1 = ((s8[4718592]{0:T(1024)(128)(4,1)}), s8[524288]{0:T(1024)(128)(4,1)S(1)}, s32[]{:S(2)}) async-start(s8[4718592]{0:T(1024)(128)(4,1)} %bitcast.52), calls=%async_computation.7 | async-start | bytes 1048576
  91.1 13.3 %collective-permute-start = (bf16[360,3072]{1,0:T(8,128)(2,1)}, bf16[360,3072]{1,0:T(8,128)(2,1)}, u32[]{:S(2)}, u32[]{:S(2)}) collective-permute-start(bf16[360,3072]{1,0:T(8,128)(2,1)} %get-tuple-element.68), channel_id=1, source_target_pairs={{0,1},{1,0},{2,3},{3,2},{4,5},{5,4},{6,7},{7,6},{8,9},{9,8},{10,11... | collective-permute-start | bytes 6635528 | tf_op jit(solution)/shard_map/ppermute | solution.py:478
  91.5 12.8 %collective-permute-start.1 = (bf16[360,768]{1,0:T(8,128)(2,1)S(1)}, bf16[360,768]{1,0:T(8,128)(2,1)S(1)}, u32[]{:S(2)}, u32[]{:S(2)}) collective-permute-start(bf16[360,768]{1,0:T(8,128)(2,1)S(1)} %broadcast_select_fusion.1), channel_id=1, source_target_pairs={{0,1},{1,0},{2,3},{3,2},{4,5},{5,4},{6,7},{7,6},{8,9},{9,8},{10,11... | collective-permute-start | bytes 1658888 | tf_op jit(solution)/shard_map/ppermute | solution.py:478
  100.4 18.0 %all-to-all-start.3 = ((bf16[128,4,384]{2,1,0:T(4,128)(2,1)}), bf16[128,4,384]{2,1,0:T(4,128)(2,1)S(1)}, u32[]{:S(2)}, u32[]{:S(2)}) async-start(bf16[128,4,384]{2,1,0:T(4,128)(2,1)} %get-tuple-element.66), calls=%async_computation.3 | async-start | bytes 786432 | tf_op jit(solution)/shard_map/all_to_all | solution.py:23
  128.0 9.8 %copy-start.11 = (bf16[8,48,768]{2,1,0:T(8,128)(2,1)S(1)}, bf16[8,48,768]{2,1,0:T(8,128)(2,1)}, u32[]{:S(2)}) copy-start(bf16[8,48,768]{2,1,0:T(8,128)(2,1)} %get-tuple-element.70) | copy-start | bytes 1769476
  128.0 11.3 %copy-start.10 = (bf16[8,48,768]{2,1,0:T(8,128)(2,1)S(1)}, bf16[8,48,768]{2,1,0:T(8,128)(2,1)}, u32[]{:S(2)}) copy-start(bf16[8,48,768]{2,1,0:T(8,128)(2,1)} %get-tuple-element.71) | copy-start | bytes 1769476
  128.0 33.7 %all-to-all-start.4 = ((bf16[128,8,384]{2,1,0:T(8,128)(2,1)}), bf16[128,8,384]{2,1,0:T(8,128)(2,1)S(1)}, u32[]{:S(2)}, u32[]{:S(2)}) async-start(bf16[128,8,384]{2,1,0:T(8,128)(2,1)} %shard_map.263), calls=%async_computation.4 | async-start | bytes 1572864 | tf_op jit(solution)/shard_map/all_to_all | solution.py:23
  137.8 17.9 %collective-permute-start.2 = (bf16[8,48,768]{2,1,0:T(8,128)(2,1)S(1)}, bf16[8,48,768]{2,1,0:T(8,128)(2,1)S(1)}, u32[]{:S(2)}, u32[]{:S(2)}) collective-permute-start(bf16[8,48,768]{2,1,0:T(8,128)(2,1)S(1)} %copy-done.11), channel_id=1, source_target_pairs={{0,64},{1,5},{2,66},{3,7},{4,68},{5,9},{6,70},{7,11},{8,72},{9,13}... | collective-permute-start | bytes 1769480 | tf_op jit(solution)/shard_map/ppermute | solution.py:683
  139.3 16.5 %collective-permute-start.3 = (bf16[8,48,768]{2,1,0:T(8,128)(2,1)S(1)}, bf16[8,48,768]{2,1,0:T(8,128)(2,1)S(1)}, u32[]{:S(2)}, u32[]{:S(2)}) collective-permute-start(bf16[8,48,768]{2,1,0:T(8,128)(2,1)S(1)} %copy-done.10), channel_id=1, source_target_pairs={{0,66},{1,13},{2,64},{3,15},{4,70},{5,1},{6,68},{7,3},{8,74},{9,5}... | collective-permute-start | bytes 1769480 | tf_op jit(solution)/shard_map/ppermute | solution.py:684
  159.0 19.5 %collective-permute-start.4 = (bf16[16,48,768]{2,1,0:T(8,128)(2,1)}, bf16[16,48,768]{2,1,0:T(8,128)(2,1)S(1)}, u32[]{:S(2)}, u32[]{:S(2)}) collective-permute-start(bf16[16,48,768]{2,1,0:T(8,128)(2,1)} %get-tuple-element.79), channel_id=1, source_target_pairs={{0,64},{1,5},{2,66},{3,7},{4,68},{5,9},{6,70},{7,11},{8,72},{9,13}... | collective-permute-start | bytes 3538952 | tf_op jit(solution)/shard_map/ppermute | solution.py:716
  159.2 20.7 %collective-permute-start.5 = (bf16[16,48,768]{2,1,0:T(8,128)(2,1)}, bf16[16,48,768]{2,1,0:T(8,128)(2,1)}, u32[]{:S(2)}, u32[]{:S(2)}) collective-permute-start(bf16[16,48,768]{2,1,0:T(8,128)(2,1)} %get-tuple-element.80), channel_id=1, source_target_pairs={{0,66},{1,13},{2,64},{3,15},{4,70},{5,1},{6,68},{7,3},{8,74},{9,5}... | collective-permute-start | bytes 3538952 | tf_op jit(solution)/shard_map/ppermute | solution.py:717
  163.0 38.8 %all-to-all-start.5 = ((bf16[128,8,384]{2,1,0:T(8,128)(2,1)}), bf16[128,8,384]{2,1,0:T(8,128)(2,1)S(1)}, u32[]{:S(2)}, u32[]{:S(2)}) async-start(bf16[128,8,384]{2,1,0:T(8,128)(2,1)} %broadcast_in_dim.32), calls=%async_computation.5 | async-start | bytes 1572864 | tf_op jit(solution)/shard_map/all_to_all | solution.py:23
  182.3 9.5 %collective-permute-start.6 = (bf16[4,48,768]{2,1,0:T(8,128)(2,1)S(1)}, bf16[4,48,768]{2,1,0:T(8,128)(2,1)S(1)}, u32[]{:S(2)}, u32[]{:S(2)}) collective-permute-start(bf16[4,48,768]{2,1,0:T(8,128)(2,1)S(1)} %get-tuple-element.81), channel_id=1, source_target_pairs={{0,4},{1,17},{2,6},{3,19},{4,8},{5,21},{6,10},{7,23},{8,12},{9,25}... | collective-permute-start | bytes 884744 | tf_op jit(solution)/shard_map/ppermute | solution.py:458
  183.2 11.9 %collective-permute-start.7 = (bf16[4,48,768]{2,1,0:T(8,128)(2,1)S(1)}, bf16[4,48,768]{2,1,0:T(8,128)(2,1)S(1)}, u32[]{:S(2)}, u32[]{:S(2)}) collective-permute-start(bf16[4,48,768]{2,1,0:T(8,128)(2,1)S(1)} %get-tuple-element.82), channel_id=1, source_target_pairs={{0,8},{1,33},{2,10},{3,35},{4,12},{5,37},{6,14},{7,39},{8,0},{9,41... | collective-permute-start | bytes 884744 | tf_op jit(solution)/shard_map/ppermute | solution.py:458
  186.8 8.2 %collective-permute-start.8 = (bf16[4,48,768]{2,1,0:T(8,128)(2,1)S(1)}, bf16[4,48,768]{2,1,0:T(8,128)(2,1)S(1)}, u32[]{:S(2)}, u32[]{:S(2)}) collective-permute-start(bf16[4,48,768]{2,1,0:T(8,128)(2,1)S(1)} %get-tuple-element.83), channel_id=1, source_target_pairs={{0,12},{1,49},{2,14},{3,51},{4,0},{5,53},{6,2},{7,55},{8,4},{9,57}... | collective-permute-start | bytes 884744 | tf_op jit(solution)/shard_map/ppermute | solution.py:458
  195.8 7.9 %collective-permute-start.10 = (bf16[48,768]{1,0:T(8,128)(2,1)S(1)}, bf16[48,768]{1,0:T(8,128)(2,1)S(1)}, u32[]{:S(2)}, u32[]{:S(2)}) collective-permute-start(bf16[48,768]{1,0:T(8,128)(2,1)S(1)} %get-tuple-element.91), channel_id=1, source_target_pairs={{0,32},{1,3},{2,34},{3,1},{4,36},{5,7},{6,38},{7,5},{8,40},{9,11},... | collective-permute-start | bytes 221192 | tf_op jit(solution)/shard_map/ppermute | solution.py:458
  200.3 3.3 %collective-permute-start.11 = (bf16[48,768]{1,0:T(8,128)(2,1)S(1)}, bf16[48,768]{1,0:T(8,128)(2,1)S(1)}, u32[]{:S(2)}, u32[]{:S(2)}) collective-permute-start(bf16[48,768]{1,0:T(8,128)(2,1)S(1)} %get-tuple-element.92), channel_id=1, source_target_pairs={{0,48},{1,67},{2,50},{3,65},{4,52},{5,71},{6,54},{7,69},{8,56},{9,... | collective-permute-start | bytes 221192 | tf_op jit(solution)/shard_map/ppermute | solution.py:458
  200.6 4.4 %collective-permute-start.9 = (bf16[48,768]{1,0:T(8,128)(2,1)S(1)}, bf16[48,768]{1,0:T(8,128)(2,1)S(1)}, u32[]{:S(2)}, u32[]{:S(2)}) collective-permute-start(bf16[48,768]{1,0:T(8,128)(2,1)S(1)} %get-tuple-element.90), channel_id=1, source_target_pairs={{0,16},{1,65},{2,18},{3,67},{4,20},{5,69},{6,22},{7,71},{8,24},{9,... | collective-permute-start | bytes 221192 | tf_op jit(solution)/shard_map/ppermute | solution.py:458
  205.6 3.5 %collective-permute-start.12 = (f32[24,768]{1,0:T(8,128)S(1)}, f32[24,768]{1,0:T(8,128)S(1)}, u32[]{:S(2)}, u32[]{:S(2)}) collective-permute-start(f32[24,768]{1,0:T(8,128)S(1)} %get-tuple-element.97), channel_id=1, source_target_pairs={{0,1},{1,0},{2,3},{3,2},{4,5},{5,4},{6,7},{7,6},{8,9},{9,8},{10,11... | collective-permute-start | bytes 221192 | tf_op jit(solution)/shard_map/ppermute | solution.py:478

commit v3 on v2

--- a/solution.py
+++ b/solution.py
@@ -170,10 +170,11 @@
 
 
 def mix(real, imag, weights, index):
-    both = (weights[0, index], weights[1, index])
-    first, second = dot3(split(real), both), dot3(split(imag), both)
-    n = first.shape[1] // 2
-    return first[:, :n] - second[:, n:], first[:, n:] + second[:, :n]
+    n = weights.shape[3] // 2
+    wr = (weights[0, index, :, :n], weights[1, index, :, :n])
+    wi = (weights[0, index, :, n:], weights[1, index, :, n:])
+    real, imag = split(real), split(imag)
+    return dot3(real, wr) - dot3(imag, wi), dot3(real, wi) + dot3(imag, wr)
 
 
 def beside(left, right):

time: 211 us -> 211 us (level)
  no operation moved by 1% of the time
where the time goes in v3:
time: 211 us; the launch traced here: 209 us
  Pallas kernels  65.3 us (31%)
  starting transfers between devices  62.4 us (30%)
  waiting for transfers between devices  57.3 us (27%)
  other arithmetic  11 us (5%)
  local copies, waits for them, and re-layouts  8.42 us (4%)
  matrix products  3.62 us (2%)
    pallas_call x13, Pallas kernels, call(): pl.pallas_call(kernel, out_shape=[(jax.ShapeDtypeStruct if i in free_outs...  65.3 us
    all_to_all x6, starting transfers between devices, exchange(): return lax.all_to_all(values, axes, split_axis=0, concat_axis=0, tiled=True)  42.1 us
    all_to_all x6, waiting for transfers between devices, exchange(): return lax.all_to_all(values, axes, split_axis=0, concat_axis=0, tiled=True)  27.5 us
    ppermute x1, waiting for transfers between devices, local(): near = lax.ppermute(sent[1], EVERY, neighbours(0, 1))  15 us
    ppermute x6, starting transfers between devices, send_all(): lax.ppermute(pieces[r], EVERY, neighbours(stage, r + 1))  11.7 us
    ppermute x1, waiting for transfers between devices, local(): lax.ppermute(plus, EVERY, neighbours(0, 1))  7.75 us
    ppermute x6, waiting for transfers between devices, send_all(): lax.ppermute(pieces[r], EVERY, neighbours(stage, r + 1))  4.71 us
  transfers between devices with their start and end apart: 19, of which 9 were waited for; matrix products, arithmetic and copies ran while one was open for 8% of the time, Pallas kernels for 14%

profile of v3, /device:TPU:1, one launch (start us, length us, event | category | flops | bytes accessed | tf_op | source)
XLA Modules:
  0.0 209.2 jit_solution(5702942189722436457)
XLA Ops:
  0.7 12.8 %all-to-all-start = ((bf16[64,2,2160]{2,1,0:T(2,128)(2,1)}), bf16[64,2,2160]{2,1,0:T(2,128)(2,1)}, u32[]{:S(2)}, u32[]{:S(2)}) async-start(bf16[64,2,2160]{2,1,0:T(2,128)(2,1)} %bitcast.50), calls=%async_computation | async-start | bytes 1114112 | tf_op jit(solution)/shard_map/all_to_all | solution.py:23
  13.5 1.1 constant_dynamic-slice_fusion
  14.6 1.3 maximum_select_fusion
  16.6 2.0 sort.17
  19.4 1.4 fusion
  20.8 7.2 %all-to-all-done = bf16[64,2,2160]{2,1,0:T(2,128)(2,1)} async-done(((bf16[64,2,2160]{2,1,0:T(2,128)(2,1)}), bf16[64,2,2160]{2,1,0:T(2,128)(2,1)}, u32[]{:S(2)}, u32[]{:S(2)}) %all-to-all-start) | async-done | bytes 552992 | tf_op jit(solution)/shard_map/all_to_all | solution.py:23
  28.0 2.8 %gather_fusion = bf16[64,2,2160]{2,1,0:T(2,128)(2,1)S(1)} fusion(bf16[64,2,2160]{2,1,0:T(2,128)(2,1)} %all-to-all-done, s32[1024]{0:T(1024)S(1)} %pad_clamp_fusion), kind=kCustom, calls=%fused_computation | custom fusion | bytes 1106176 | tf_op jit(solution)/shard_map/jit(_take)/gather | solution.py:587
  31.4 1.1 reshape.158.base_ref
  32.5 3.2 %shard_map.257 = (bf16[128,4,384]{2,1,0:T(4,128)(2,1)}, f32[360,768]{1,0:T(8,128)}, f32[360,128]{1,0:T(8,128)}) custom-call(f32[360,768]{1,0:T(8,128)S(1)} %reshape.158.base_ref, bf16[2,256,360]{2,1,0:T(8,128)(2,1)} %constant.80.clone.table_ref), custom_call_target="tpu_custom_call" | custom-call | tf_op jit(solution)/shard_map/pallas_call | solution.py:328
  35.7 3.9 %all-to-all-start.1 = ((bf16[128,4,384]{2,1,0:T(4,128)(2,1)}), bf16[128,4,384]{2,1,0:T(4,128)(2,1)S(1)}, u32[]{:S(2)}, u32[]{:S(2)}) async-start(bf16[128,4,384]{2,1,0:T(4,128)(2,1)} %get-tuple-element.59), calls=%async_computation.1 | async-start | bytes 786432 | tf_op jit(solution)/shard_map/all_to_all | solution.py:23
  39.6 0.7 fusion.2.vectors_ref
  40.3 1.6 subtract_convert_fusion
  42.0 1.6 pad_maximum_fusion.1.weights_ref
  43.6 8.7 %all-to-all-done.1.rows_ref = bf16[128,4,384]{2,1,0:T(4,128)(2,1)S(1)} async-done(((bf16[128,4,384]{2,1,0:T(4,128)(2,1)}), bf16[128,4,384]{2,1,0:T(4,128)(2,1)S(1)}, u32[]{:S(2)}, u32[]{:S(2)}) %all-to-all-start.1) | async-done | bytes 393248 | tf_op jit(solution)/shard_map/all_to_all | solution.py:23
  52.2 6.6 %shard_map.258 = (bf16[128,4,384]{2,1,0:T(4,128)(2,1)}, f32[2,256,384]{2,1,0:T(8,128)}, f32[2,256,384]{2,1,0:T(8,128)}) custom-call(bf16[128,4,384]{2,1,0:T(4,128)(2,1)S(1)} %all-to-all-done.1.rows_ref, bf16[2,256,256]{2,1,0:T(8,128)(2,1)} %constant.81.clone.table_ref, bf16[2,256,256]{2,1,0:T(8,128)(2,1)} %constant.82.clone.turned_ref, ...), custom_call_target="tpu_custom_call" | custom-call | tf_op jit(solution)/shard_map/pallas_call | solution.py:328
  58.8 3.9 %all-to-all-start.2 = ((bf16[128,4,384]{2,1,0:T(4,128)(2,1)}), bf16[128,4,384]{2,1,0:T(4,128)(2,1)S(1)}, u32[]{:S(2)}, u32[]{:S(2)}) async-start(bf16[128,4,384]{2,1,0:T(4,128)(2,1)} %get-tuple-element.60), calls=%async_computation.2 | async-start | bytes 786432 | tf_op jit(solution)/shard_map/all_to_all | solution.py:23
  63.7 11.7 %all-to-all-done.2.rows_ref = bf16[128,4,384]{2,1,0:T(4,128)(2,1)S(1)} async-done(((bf16[128,4,384]{2,1,0:T(4,128)(2,1)}), bf16[128,4,384]{2,1,0:T(4,128)(2,1)S(1)}, u32[]{:S(2)}, u32[]{:S(2)}) %all-to-all-start.2) | async-done | bytes 393248 | tf_op jit(solution)/shard_map/all_to_all | solution.py:23
  75.4 3.7 %shard_map.259 = (bf16[360,768]{1,0:T(8,128)(2,1)S(1)}, f32[360,768]{1,0:T(8,128)}, f32[360,128]{1,0:T(8,128)}) custom-call(bf16[128,4,384]{2,1,0:T(4,128)(2,1)S(1)} %all-to-all-done.2.rows_ref, bf16[2,360,256]{2,1,0:T(8,128)(2,1)} %constant.83.clone.table_ref, f32[360,768]{1,0:T(8,128)} %copy-done, f32[360,768]{1,0:T(8,128)} %get-tuple-element.61.xhat_ref, ...), custom_call_target="tpu_custom_call" | custom-call | tf_op jit(solution)/shard_map/pallas_call | solution.py:328
  79.1 11.4 %shard_map.260 = (bf16[360,3072]{1,0:T(8,128)(2,1)}, bf16[360,3072]{1,0:T(8,128)(2,1)}, bf16[360,3072]{1,0:T(8,128)(2,1)}, f32[8,1,384]{2,1,0:T(1,128)S(1)}) custom-call(s32[7]{0:T(128)S(1)} %stack.52.place_ref.refs_0_, bf16[360,768]{1,0:T(8,128)(2,1)S(1)} %get-tuple-element.62.flat_ref, bf16[360,768]{1,0:T(8,128)(2,1)S(1)} %reshape.154.cot_ref, ...), custom_call_target="tpu_custom_call" | custom-call | flops 3397386240 | bytes 18874368 | tf_op jit(solution)/shard_map/pallas_call | solution.py:328
  91.2 3.6 %fusion.8.grad_ref = f32[360,768]{1,0:T(8,128)S(1)} fusion(bf16[360,3072]{1,0:T(8,128)(2,1)} %get-tuple-element.63.grad_ref, bf16[768,3072]{1,0:T(8,128)(2,1)S(1)} %bitcast.53), kind=kOutput, calls=%fused_computation.46 | convolution fusion | flops 1698693120 | bytes 8036352 | tf_op jit(solution)/shard_map/tf,df->td/dot_general | solution.py:665
  94.8 4.3 %shard_map.261 = (bf16[128,4,384]{2,1,0:T(4,128)(2,1)}, f32[360,768]{1,0:T(8,128)}, f32[3,768]{1,0:T(4,128)}) custom-call(f32[360,768]{1,0:T(8,128)S(1)} %fusion.8.grad_ref, bf16[360,768]{1,0:T(8,128)(2,1)S(1)} %reshape.154.cot_ref, f32[360,768]{1,0:T(8,128)} %get-tuple-element.64.xhat2_ref, f32[360,128]{1,0:T(8,128)} %get-tuple-element.65.rstd2_ref, ...), custom_call_target="tpu_custom_call" | custom-call | tf_op jit(solution)/shard_map/pallas_call | solution.py:328
  99.1 0.7 reshape.157
  99.9 3.9 %all-to-all-start.3 = ((bf16[128,4,384]{2,1,0:T(4,128)(2,1)}), bf16[128,4,384]{2,1,0:T(4,128)(2,1)S(1)}, u32[]{:S(2)}, u32[]{:S(2)}) async-start(bf16[128,4,384]{2,1,0:T(4,128)(2,1)} %get-tuple-element.66), calls=%async_computation.3 | async-start | bytes 786432 | tf_op jit(solution)/shard_map/all_to_all | solution.py:23
  103.8 14.1 %shard_map.262 = (f32[16,48,768]{2,1,0:T(8,128)}, bf16[16,48,768]{2,1,0:T(8,128)(2,1)}, bf16[8,48,768]{2,1,0:T(8,128)(2,1)}, bf16[8,48,768]{2,1,0:T(8,128)(2,1)}, bf16[16,48,768]{2,1,0:T(8,128)(2,1)}) custom-call(s32[7]{0:T(128)S(1)} %stack.52.place_ref.refs_0_, bf16[360,3072]{1,0:T(8,128)(2,1)} %get-tuple-element.63.grad_ref, ...), custom_call_target="tpu_custom_call" | custom-call | flops 3397386240 | bytes 14680064 | tf_op jit(solution)/shard_map/pallas_call | solution.py:328
  117.9 9.6 %shard_map.263 = bf16[128,8,384]{2,1,0:T(8,128)(2,1)} custom-call(bf16[128,4,384]{2,1,0:T(4,128)(2,1)S(1)} %all-to-all-done.3.rows_ref, bf16[2,256,256]{2,1,0:T(8,128)(2,1)} %constant.81.clone.table_ref, bf16[2,256,256]{2,1,0:T(8,128)(2,1)} %constant.82.clone.turned_ref, bf16[2,2,384,768]{3,2,1,0:T(8,128)(2,1)} %pad_maximum_fusion.1.weights_ref, ...), custom_call_target="tpu_custom_call" | custom-call | tf_op jit(solution)/shard_map/pallas_call | solution.py:328
  127.4 9.8 %all-to-all-start.4 = ((bf16[128,8,384]{2,1,0:T(8,128)(2,1)}), bf16[128,8,384]{2,1,0:T(8,128)(2,1)S(1)}, u32[]{:S(2)}, u32[]{:S(2)}) async-start(bf16[128,8,384]{2,1,0:T(8,128)(2,1)} %shard_map.263), calls=%async_computation.4 | async-start | bytes 1572864 | tf_op jit(solution)/shard_map/all_to_all | solution.py:23
  137.3 1.4 collective-permute-start.2
  138.7 1.4 collective-permute-start.3
  140.2 15.0 %collective-permute-done.2.near_ref = bf16[8,48,768]{2,1,0:T(8,128)(2,1)S(1)} collective-permute-done((bf16[8,48,768]{2,1,0:T(8,128)(2,1)S(1)}, bf16[8,48,768]{2,1,0:T(8,128)(2,1)S(1)}, u32[]{:S(2)}, u32[]{:S(2)}) %collective-permute-start.2) | collective-permute-done | bytes 589856 | tf_op jit(solution)/shard_map/ppermute | solution.py:684
  155.2 3.3 %shard_map.264 = (bf16[16,48,768]{2,1,0:T(8,128)(2,1)}, bf16[16,48,768]{2,1,0:T(8,128)(2,1)}) custom-call(bf16[16,48,768]{2,1,0:T(8,128)(2,1)} %get-tuple-element.69.out1_ref, bf16[16,48,768]{2,1,0:T(8,128)(2,1)} %get-tuple-element.72.out3_ref, bf16[8,48,768]{2,1,0:T(8,128)(2,1)S(1)} %collective-permute-done.2.near_ref, ...), custom_call_target="tpu_custom_call" | custom-call | tf_op jit(solution)/shard_map/pallas_call | solution.py:328
  158.6 2.5 %collective-permute-start.5 = (bf16[16,48,768]{2,1,0:T(8,128)(2,1)}, bf16[16,48,768]{2,1,0:T(8,128)(2,1)}, u32[]{:S(2)}, u32[]{:S(2)}) collective-permute-start(bf16[16,48,768]{2,1,0:T(8,128)(2,1)} %get-tuple-element.80), channel_id=1, source_target_pairs={{0,66},{1,13},{2,64},{3,15},{4,70},{5,1},{6,68},{7,3},{8,74},{9,5}... | collective-permute-start | bytes 3538952 | tf_op jit(solution)/shard_map/ppermute | solution.py:718
  161.5 1.0 broadcast_in_dim.32
  162.5 7.8 %all-to-all-start.5 = ((bf16[128,8,384]{2,1,0:T(8,128)(2,1)}), bf16[128,8,384]{2,1,0:T(8,128)(2,1)S(1)}, u32[]{:S(2)}, u32[]{:S(2)}) async-start(bf16[128,8,384]{2,1,0:T(8,128)(2,1)} %broadcast_in_dim.32), calls=%async_computation.5 | async-start | bytes 1572864 | tf_op jit(solution)/shard_map/all_to_all | solution.py:23
  170.2 7.7 %collective-permute-done.4.refs_0_ = bf16[16,48,768]{2,1,0:T(8,128)(2,1)S(1)} collective-permute-done((bf16[16,48,768]{2,1,0:T(8,128)(2,1)}, bf16[16,48,768]{2,1,0:T(8,128)(2,1)S(1)}, u32[]{:S(2)}, u32[]{:S(2)}) %collective-permute-start.4) | collective-permute-done | bytes 1179680 | tf_op jit(solution)/shard_map/ppermute | solution.py:717
  178.0 1.4 collective-permute-done.5.refs_1_
  179.4 2.3 %shard_map.265 = (f32[4,48,768]{2,1,0:T(8,128)S(1)}, bf16[4,48,768]{2,1,0:T(8,128)(2,1)S(1)}, bf16[4,48,768]{2,1,0:T(8,128)(2,1)S(1)}, bf16[4,48,768]{2,1,0:T(8,128)(2,1)S(1)}) custom-call(s32[7]{0:T(128)S(1)} %stack.52.place_ref.refs_0_, f32[16,48,768]{2,1,0:T(8,128)} %get-tuple-element.78.own_in_ref, ...), custom_call_target="tpu_custom_call" | custom-call | tf_op jit(solution)/shard_map/pallas_call | solution.py:328
  181.7 0.9 collective-permute-start.6
  182.7 3.6 %collective-permute-start.7 = (bf16[4,48,768]{2,1,0:T(8,128)(2,1)S(1)}, bf16[4,48,768]{2,1,0:T(8,128)(2,1)S(1)}, u32[]{:S(2)}, u32[]{:S(2)}) collective-permute-start(bf16[4,48,768]{2,1,0:T(8,128)(2,1)S(1)} %get-tuple-element.82), channel_id=1, source_target_pairs={{0,8},{1,33},{2,10},{3,35},{4,12},{5,37},{6,14},{7,39},{8,0},{9,41... | collective-permute-start | bytes 884744 | tf_op jit(solution)/shard_map/ppermute | solution.py:459
  186.3 1.2 collective-permute-start.8
  187.5 3.7 %shard_map.266 = f32[360,1,768]{2,1,0:T(1,128)} custom-call(bf16[128,8,384]{2,1,0:T(8,128)(2,1)S(1)} %all-to-all-done.4.rows_ref, bf16[2,360,256]{2,1,0:T(8,128)(2,1)} %constant.85.clone.table_ref, f32[360,768]{1,0:T(8,128)} %get-tuple-element.85.mixed_ref, f32[360,768]{1,0:T(8,128)} %get-tuple-element.61.xhat_ref, f32[360,128]{1,0:T(8,128)} %get-tuple-element.86.rstd_ref, ...), custom_call_target="tpu_custom_call" | custom-call | tf_op jit(solution)/shard_map/pallas_call | solution.py:328
  191.2 3.3 %collective-permute-done.7.refs_1_ = bf16[4,48,768]{2,1,0:T(8,128)(2,1)S(1)} collective-permute-done((bf16[4,48,768]{2,1,0:T(8,128)(2,1)S(1)}, bf16[4,48,768]{2,1,0:T(8,128)(2,1)S(1)}, u32[]{:S(2)}, u32[]{:S(2)}) %collective-permute-start.7) | collective-permute-done | bytes 294944 | tf_op jit(solution)/shard_map/ppermute | solution.py:459
  194.5 0.7 shard_map.267
  195.2 4.5 %collective-permute-start.10 = (bf16[48,768]{1,0:T(8,128)(2,1)S(1)}, bf16[48,768]{1,0:T(8,128)(2,1)S(1)}, u32[]{:S(2)}, u32[]{:S(2)}) collective-permute-start(bf16[48,768]{1,0:T(8,128)(2,1)S(1)} %get-tuple-element.91), channel_id=1, source_target_pairs={{0,32},{1,3},{2,34},{3,1},{4,36},{5,7},{6,38},{7,5},{8,40},{9,11},... | collective-permute-start | bytes 221192 | tf_op jit(solution)/shard_map/ppermute | solution.py:459
  200.0 1.2 collective-permute-start.9
  201.2 1.9 shard_map.268
  203.1 1.4 collective-permute-done.9.refs_2_
  205.0 2.6 %collective-permute-start.12 = (f32[24,768]{1,0:T(8,128)S(1)}, f32[24,768]{1,0:T(8,128)S(1)}, u32[]{:S(2)}, u32[]{:S(2)}) collective-permute-start(f32[24,768]{1,0:T(8,128)S(1)} %get-tuple-element.97), channel_id=1, source_target_pairs={{0,1},{1,0},{2,3},{3,2},{4,5},{5,4},{6,7},{7,6},{8,9},{9,8},{10,11... | collective-permute-start | bytes 221192 | tf_op jit(solution)/shard_map/ppermute | solution.py:479
  207.6 0.9 collective-permute-done.12
  (73 shorter events, 5.9 us)
Async XLA Ops:
  0.6 12.8 %copy-start.5 = (f32[2,8,96,96]{3,2,1,0:T(8,128)S(1)}, f32[2,8,96,96]{3,2,1,0:T(8,128)}, u32[]{:S(2)}) copy-start(f32[2,8,96,96]{3,2,1,0:T(8,128)} %param.23) | copy-start | bytes 1769476
  0.7 27.3 %all-to-all-start = ((bf16[64,2,2160]{2,1,0:T(2,128)(2,1)}), bf16[64,2,2160]{2,1,0:T(2,128)(2,1)}, u32[]{:S(2)}, u32[]{:S(2)}) async-start(bf16[64,2,2160]{2,1,0:T(2,128)(2,1)} %bitcast.50), calls=%async_computation | async-start | bytes 1114112 | tf_op jit(solution)/shard_map/all_to_all | solution.py:23
  15.9 0.7 copy-start.12
  18.6 0.7 copy-start.8
  19.4 1.4 copy-start.2
  32.5 9.4 %copy-start = (f32[360,768]{1,0:T(8,128)}, f32[360,768]{1,0:T(8,128)S(1)}, u32[]{:S(2)}) copy-start(f32[360,768]{1,0:T(8,128)S(1)} %reshape.158.base_ref) | copy-start | bytes 3317764
  32.5 7.1 %copy-start.6 = (f32[2,768]{1,0:T(2,128)S(1)}, f32[2,768]{1,0:T(2,128)}, u32[]{:S(2)}) copy-start(f32[2,768]{1,0:T(2,128)} %param.22) | copy-start | bytes 18436
  32.5 7.1 %copy-start.7 = (f32[2,768]{1,0:T(2,128)S(1)}, f32[2,768]{1,0:T(2,128)}, u32[]{:S(2)}) copy-start(f32[2,768]{1,0:T(2,128)} %param.24) | copy-start | bytes 18436
  35.7 16.5 %all-to-all-start.1 = ((bf16[128,4,384]{2,1,0:T(4,128)(2,1)}), bf16[128,4,384]{2,1,0:T(4,128)(2,1)S(1)}, u32[]{:S(2)}, u32[]{:S(2)}) async-start(bf16[128,4,384]{2,1,0:T(4,128)(2,1)} %get-tuple-element.59), calls=%async_computation.1 | async-start | bytes 786432 | tf_op jit(solution)/shard_map/all_to_all | solution.py:23
  40.3 1.6 copy-start.3
  43.6 19.2 %copy-start.9 = (f32[768]{0:T(1024)S(1)}, f32[768]{0:T(1024)}, u32[]{:S(2)}) copy-start(f32[768]{0:T(1024)} %param.25) | copy-start | bytes 9220
  58.8 4.0 %copy-start.4 = (bf16[2,1,180,768]{3,0,2,1:T(2,128)(2,1)S(1)}, bf16[2,1,180,768]{3,0,2,1:T(2,128)(2,1)}, u32[]{:S(2)}) copy-start(bf16[2,1,180,768]{3,0,2,1:T(2,128)(2,1)} %param.29) | copy-start | bytes 1658884
  58.8 16.6 %all-to-all-start.2 = ((bf16[128,4,384]{2,1,0:T(4,128)(2,1)}), bf16[128,4,384]{2,1,0:T(4,128)(2,1)S(1)}, u32[]{:S(2)}, u32[]{:S(2)}) async-start(bf16[128,4,384]{2,1,0:T(4,128)(2,1)} %get-tuple-element.60), calls=%async_computation.2 | async-start | bytes 786432 | tf_op jit(solution)/shard_map/all_to_all | solution.py:23
  75.4 3.7 %copy-start.1 = (f32[3072]{0:T(1024)S(1)}, f32[3072]{0:T(1024)}, u32[]{:S(2)}) copy-start(f32[3072]{0:T(1024)} %param.27) | copy-start | bytes 36868
  79.1 12.1 %slice-start = ((s8[4718592]{0:T(1024)(128)(4,1)}), s8[4194304]{0:T(1024)(128)(4,1)S(1)}, s32[]{:S(2)}) async-start(s8[4718592]{0:T(1024)(128)(4,1)} %bitcast.52), calls=%async_computation.6 | async-start | bytes 8388608
  79.1 12.1 %slice-start.1 = ((s8[4718592]{0:T(1024)(128)(4,1)}), s8[524288]{0:T(1024)(128)(4,1)S(1)}, s32[]{:S(2)}) async-start(s8[4718592]{0:T(1024)(128)(4,1)} %bitcast.52), calls=%async_computation.7 | async-start | bytes 1048576
  90.5 13.3 %collective-permute-start = (bf16[360,3072]{1,0:T(8,128)(2,1)}, bf16[360,3072]{1,0:T(8,128)(2,1)}, u32[]{:S(2)}, u32[]{:S(2)}) collective-permute-start(bf16[360,3072]{1,0:T(8,128)(2,1)} %get-tuple-element.68), channel_id=1, source_target_pairs={{0,1},{1,0},{2,3},{3,2},{4,5},{5,4},{6,7},{7,6},{8,9},{9,8},{10,11... | collective-permute-start | bytes 6635528 | tf_op jit(solution)/shard_map/ppermute | solution.py:479
  91.0 12.8 %collective-permute-start.1 = (bf16[360,768]{1,0:T(8,128)(2,1)S(1)}, bf16[360,768]{1,0:T(8,128)(2,1)S(1)}, u32[]{:S(2)}, u32[]{:S(2)}) collective-permute-start(bf16[360,768]{1,0:T(8,128)(2,1)S(1)} %broadcast_select_fusion.1), channel_id=1, source_target_pairs={{0,1},{1,0},{2,3},{3,2},{4,5},{5,4},{6,7},{7,6},{8,9},{9,8},{10,11... | collective-permute-start | bytes 1658888 | tf_op jit(solution)/shard_map/ppermute | solution.py:479
  99.9 18.0 %all-to-all-start.3 = ((bf16[128,4,384]{2,1,0:T(4,128)(2,1)}), bf16[128,4,384]{2,1,0:T(4,128)(2,1)S(1)}, u32[]{:S(2)}, u32[]{:S(2)}) async-start(bf16[128,4,384]{2,1,0:T(4,128)(2,1)} %get-tuple-element.66), calls=%async_computation.3 | async-start | bytes 786432 | tf_op jit(solution)/shard_map/all_to_all | solution.py:23
  127.4 9.8 %copy-start.11 = (bf16[8,48,768]{2,1,0:T(8,128)(2,1)S(1)}, bf16[8,48,768]{2,1,0:T(8,128)(2,1)}, u32[]{:S(2)}) copy-start(bf16[8,48,768]{2,1,0:T(8,128)(2,1)} %get-tuple-element.70) | copy-start | bytes 1769476
  127.4 11.3 %copy-start.10 = (bf16[8,48,768]{2,1,0:T(8,128)(2,1)S(1)}, bf16[8,48,768]{2,1,0:T(8,128)(2,1)}, u32[]{:S(2)}) copy-start(bf16[8,48,768]{2,1,0:T(8,128)(2,1)} %get-tuple-element.71) | copy-start | bytes 1769476
  127.4 33.7 %all-to-all-start.4 = ((bf16[128,8,384]{2,1,0:T(8,128)(2,1)}), bf16[128,8,384]{2,1,0:T(8,128)(2,1)S(1)}, u32[]{:S(2)}, u32[]{:S(2)}) async-start(bf16[128,8,384]{2,1,0:T(8,128)(2,1)} %shard_map.263), calls=%async_computation.4 | async-start | bytes 1572864 | tf_op jit(solution)/shard_map/all_to_all | solution.py:23
  137.3 17.9 %collective-permute-start.2 = (bf16[8,48,768]{2,1,0:T(8,128)(2,1)S(1)}, bf16[8,48,768]{2,1,0:T(8,128)(2,1)S(1)}, u32[]{:S(2)}, u32[]{:S(2)}) collective-permute-start(bf16[8,48,768]{2,1,0:T(8,128)(2,1)S(1)} %copy-done.11), channel_id=1, source_target_pairs={{0,64},{1,5},{2,66},{3,7},{4,68},{5,9},{6,70},{7,11},{8,72},{9,13}... | collective-permute-start | bytes 1769480 | tf_op jit(solution)/shard_map/ppermute | solution.py:684
  138.7 16.5 %collective-permute-start.3 = (bf16[8,48,768]{2,1,0:T(8,128)(2,1)S(1)}, bf16[8,48,768]{2,1,0:T(8,128)(2,1)S(1)}, u32[]{:S(2)}, u32[]{:S(2)}) collective-permute-start(bf16[8,48,768]{2,1,0:T(8,128)(2,1)S(1)} %copy-done.10), channel_id=1, source_target_pairs={{0,66},{1,13},{2,64},{3,15},{4,70},{5,1},{6,68},{7,3},{8,74},{9,5}... | collective-permute-start | bytes 1769480 | tf_op jit(solution)/shard_map/ppermute | solution.py:685
  158.5 19.5 %collective-permute-start.4 = (bf16[16,48,768]{2,1,0:T(8,128)(2,1)}, bf16[16,48,768]{2,1,0:T(8,128)(2,1)S(1)}, u32[]{:S(2)}, u32[]{:S(2)}) collective-permute-start(bf16[16,48,768]{2,1,0:T(8,128)(2,1)} %get-tuple-element.79), channel_id=1, source_target_pairs={{0,64},{1,5},{2,66},{3,7},{4,68},{5,9},{6,70},{7,11},{8,72},{9,13}... | collective-permute-start | bytes 3538952 | tf_op jit(solution)/shard_map/ppermute | solution.py:717
  158.6 20.7 %collective-permute-start.5 = (bf16[16,48,768]{2,1,0:T(8,128)(2,1)}, bf16[16,48,768]{2,1,0:T(8,128)(2,1)}, u32[]{:S(2)}, u32[]{:S(2)}) collective-permute-start(bf16[16,48,768]{2,1,0:T(8,128)(2,1)} %get-tuple-element.80), channel_id=1, source_target_pairs={{0,66},{1,13},{2,64},{3,15},{4,70},{5,1},{6,68},{7,3},{8,74},{9,5}... | collective-permute-start | bytes 3538952 | tf_op jit(solution)/shard_map/ppermute | solution.py:718
  162.5 38.8 %all-to-all-start.5 = ((bf16[128,8,384]{2,1,0:T(8,128)(2,1)}), bf16[128,8,384]{2,1,0:T(8,128)(2,1)S(1)}, u32[]{:S(2)}, u32[]{:S(2)}) async-start(bf16[128,8,384]{2,1,0:T(8,128)(2,1)} %broadcast_in_dim.32), calls=%async_computation.5 | async-start | bytes 1572864 | tf_op jit(solution)/shard_map/all_to_all | solution.py:23
  181.7 9.5 %collective-permute-start.6 = (bf16[4,48,768]{2,1,0:T(8,128)(2,1)S(1)}, bf16[4,48,768]{2,1,0:T(8,128)(2,1)S(1)}, u32[]{:S(2)}, u32[]{:S(2)}) collective-permute-start(bf16[4,48,768]{2,1,0:T(8,128)(2,1)S(1)} %get-tuple-element.81), channel_id=1, source_target_pairs={{0,4},{1,17},{2,6},{3,19},{4,8},{5,21},{6,10},{7,23},{8,12},{9,25}... | collective-permute-start | bytes 884744 | tf_op jit(solution)/shard_map/ppermute | solution.py:459
  182.7 11.9 %collective-permute-start.7 = (bf16[4,48,768]{2,1,0:T(8,128)(2,1)S(1)}, bf16[4,48,768]{2,1,0:T(8,128)(2,1)S(1)}, u32[]{:S(2)}, u32[]{:S(2)}) collective-permute-start(bf16[4,48,768]{2,1,0:T(8,128)(2,1)S(1)} %get-tuple-element.82), channel_id=1, source_target_pairs={{0,8},{1,33},{2,10},{3,35},{4,12},{5,37},{6,14},{7,39},{8,0},{9,41... | collective-permute-start | bytes 884744 | tf_op jit(solution)/shard_map/ppermute | solution.py:459
  186.3 8.2 %collective-permute-start.8 = (bf16[4,48,768]{2,1,0:T(8,128)(2,1)S(1)}, bf16[4,48,768]{2,1,0:T(8,128)(2,1)S(1)}, u32[]{:S(2)}, u32[]{:S(2)}) collective-permute-start(bf16[4,48,768]{2,1,0:T(8,128)(2,1)S(1)} %get-tuple-element.83), channel_id=1, source_target_pairs={{0,12},{1,49},{2,14},{3,51},{4,0},{5,53},{6,2},{7,55},{8,4},{9,57}... | collective-permute-start | bytes 884744 | tf_op jit(solution)/shard_map/ppermute | solution.py:459
  195.2 7.9 %collective-permute-start.10 = (bf16[48,768]{1,0:T(8,128)(2,1)S(1)}, bf16[48,768]{1,0:T(8,128)(2,1)S(1)}, u32[]{:S(2)}, u32[]{:S(2)}) collective-permute-start(bf16[48,768]{1,0:T(8,128)(2,1)S(1)} %get-tuple-element.91), channel_id=1, source_target_pairs={{0,32},{1,3},{2,34},{3,1},{4,36},{5,7},{6,38},{7,5},{8,40},{9,11},... | collective-permute-start | bytes 221192 | tf_op jit(solution)/shard_map/ppermute | solution.py:459
  199.8 3.3 %collective-permute-start.11 = (bf16[48,768]{1,0:T(8,128)(2,1)S(1)}, bf16[48,768]{1,0:T(8,128)(2,1)S(1)}, u32[]{:S(2)}, u32[]{:S(2)}) collective-permute-start(bf16[48,768]{1,0:T(8,128)(2,1)S(1)} %get-tuple-element.92), channel_id=1, source_target_pairs={{0,48},{1,67},{2,50},{3,65},{4,52},{5,71},{6,54},{7,69},{8,56},{9,... | collective-permute-start | bytes 221192 | tf_op jit(solution)/shard_map/ppermute | solution.py:459
  200.0 4.4 %collective-permute-start.9 = (bf16[48,768]{1,0:T(8,128)(2,1)S(1)}, bf16[48,768]{1,0:T(8,128)(2,1)S(1)}, u32[]{:S(2)}, u32[]{:S(2)}) collective-permute-start(bf16[48,768]{1,0:T(8,128)(2,1)S(1)} %get-tuple-element.90), channel_id=1, source_target_pairs={{0,16},{1,65},{2,18},{3,67},{4,20},{5,69},{6,22},{7,71},{8,24},{9,... | collective-permute-start | bytes 221192 | tf_op jit(solution)/shard_map/ppermute | solution.py:459
  205.0 3.5 %collective-permute-start.12 = (f32[24,768]{1,0:T(8,128)S(1)}, f32[24,768]{1,0:T(8,128)S(1)}, u32[]{:S(2)}, u32[]{:S(2)}) collective-permute-start(f32[24,768]{1,0:T(8,128)S(1)} %get-tuple-element.97), channel_id=1, source_target_pairs={{0,1},{1,0},{2,3},{3,2},{4,5},{5,4},{6,7},{7,6},{8,9},{9,8},{10,11... | collective-permute-start | bytes 221192 | tf_op jit(solution)/shard_map/ppermute | solution.py:479
